TPU v7x, 256 devices: a whole 4x4x8 slice. The times are simulated.
256 devices in a mesh: segment: 8 (over z), tile: 32 (over x, y, core).
Axes of the slice: x: 4, y: 4, z: 8, core: 2. Of those that a mesh axis runs over, the one named last changes fastest.
Arguments:
- latent: bfloat16 [4, 8, 128, 384], P(None, None, 'tile'), may hold values from -6 to 6
- frame_order: int32 [4], replicated, may hold values from 0 to 3, each once
- section_weight: bfloat16 [8, 27, 384, 384], P('segment'), may hold values from -0.0625 to 0.0625
- section_gain: bfloat16 [8, 384], P('segment'), may hold values from 0.5 to 1.5
- up_weight: bfloat16 [27, 384, 192], P(None, 'tile'), may hold values from -0.0625 to 0.0625
- reward_weight: bfloat16 [49152, 1280], P(None, 'tile'), may hold values from -0.02734375 to 0.02734375
- reward_coef: float32 [1280], P('tile'), may hold values from -6 to 6
Outputs:
- input_grads: float32 [8, 4, 8, 128, 384], P('segment', None, None, 'tile')
All inputs are finite; a program needn't handle non-finite values.
Results may differ from a plain program's by a relative error of at most 0.03.
Values may be sent and summed in bfloat16 or wider, within the bound.
No kernel may reach another device: no remote copies, remote signals or barrier semaphores. Data moves between devices by JAX's collectives and lax.ppermute only.
A program may use at most 128 MiB of HBM per device.

v0:
```python
import functools

import jax
import jax.numpy as jnp
from jax import lax
from jax.experimental import pallas as pl
from jax.experimental.pallas import tpu as pltpu
from jax.sharding import PartitionSpec as P

EPS = 1e-06
F32 = jnp.float32
BF16 = jnp.bfloat16
AXES = ("segment", "chip", "core")
TILE = ("chip", "core")
PAD = 16
VM = pl.BlockSpec(memory_space=pltpu.VMEM)
HB = pl.BlockSpec(memory_space=pl.ANY)
SM = pl.BlockSpec(memory_space=pltpu.SMEM)
GRANT = pltpu.CompilerParams(vmem_limit_bytes=24 * 2**20)


def row_shifts(v):
    count = v.shape[0]
    row = lax.broadcasted_iota(jnp.int32, v.shape, 0) & 7
    before = jnp.where(row == 0, 0.0, pltpu.roll(v, 1, 0))
    after = jnp.where(row == 7, 0.0, pltpu.roll(v, count - 1, 0))
    return before, after


PIECES = 6


def weight_copy(w_hbm, w_buf, sem, piece):
    rows = w_hbm.shape[0] // PIECES
    part = pl.ds(pl.multiple_of(piece * rows, 64), rows)
    return pltpu.make_async_copy(w_hbm.at[part], w_buf.at[part], sem.at[piece])


def start_weights(w_hbm, w_buf, sem, backward):
    per = PIECES // 3
    for step in range(PIECES):
        a = 2 - step // per if backward else step // per
        weight_copy(w_hbm, w_buf, sem, a * per + step % per).start()


def convolve(taps, w_hbm, w_buf, sem, acc_ref, backward):
    count = acc_ref.shape[0]
    block = count // 4
    per = PIECES // 3
    rows = w_hbm.shape[0] // PIECES
    acc_ref[...] = jnp.zeros_like(acc_ref)

    @pl.loop(0, 3)
    def _(step):
        a = 2 - step if backward else step
        for part in range(per):
            piece = a * per + part
            weight_copy(w_hbm, w_buf, sem, piece).wait()
            acc_ref[...] += jnp.dot(
                taps[pl.ds(pl.multiple_of(step * block, 16), count), part * rows : (part + 1) * rows],
                w_buf[pl.ds(pl.multiple_of(piece * rows, 64), rows), :],
                preferred_element_type=F32,
            )


def column_block(pieces, t):
    parts = [piece[t] for piece in pieces]
    return parts[0] if len(parts) == 1 else jnp.concatenate(parts, axis=0)


def write_block(out, refs, t):
    cols = out.shape[0]
    if len(refs) == 2:
        refs[0][t] = out[:3]
        refs[1][t] = out[cols - 3 :]
    else:
        edge = refs[1].shape[1]
        refs[0][t] = out
        refs[1][t] = out[:edge]
        refs[2][t] = out[cols - edge :]


def edge_scales(form, tile_ref, dtype):
    one, none = jnp.ones((), dtype), jnp.zeros((), dtype)
    low = jnp.where(tile_ref[0] == 0, none, one) if form == "even" else one
    high = jnp.where(tile_ref[0] == tile_ref[1] - 1, none, one)
    return low, high


def put_taps(taps, t_at, v, b, columns, ch, cut, backward):
    rows = 8
    block = columns * rows
    for c in range(3):
        start = (2 - c if backward else c) * rows
        piece = v[start : start + block]
        if cut is not None and c != 1:
            bad = (2 if start == 0 else 1) * rows
            piece = jnp.concatenate([piece[:bad], piece[bad : bad + rows] * cut, piece[bad + rows :]], axis=0)
        at = (3 * b + c) * ch
        taps[pl.ds(pl.multiple_of(t_at * block, 16), block), at : at + ch] = piece.astype(BF16)


def fwd_kernel(form, count, *refs):
    tile_ref, *pieces = refs[: count + 1]
    gain_ref, w_hbm = refs[count + 1 : count + 3]
    *outs, taps, w_buf, acc, sem = refs[count + 3 :]
    start_weights(w_hbm, w_buf, sem, False)
    frames, _, rows, ch = pieces[0].shape
    outer = sum(piece.shape[1] for piece in pieces)
    inner = outer - 2
    block = inner * rows
    gain = gain_ref[...].astype(F32)
    low, high = edge_scales(form, tile_ref, F32)
    taps[0 : 2 * block, :] = jnp.zeros((2 * block, 9 * ch), BF16)
    @pl.loop(0, frames)
    def _(t):
        x = column_block(pieces, t).astype(F32)
        if form == "even":
            x = jnp.concatenate([x[:1] * low, x[1:-1], x[-1:] * high], axis=0)
        x = x.reshape(outer * rows, ch)
        inv = lax.rsqrt(jnp.mean(x * x, axis=-1, keepdims=True) + EPS)
        act = jax.nn.silu(x * inv * gain)
        before, after = row_shifts(act)
        for b, v in enumerate((before, act, after)):
            put_taps(taps, 2 + t, v, b, inner, ch, high if form == "odd" else None, False)
    convolve(taps, w_hbm, w_buf, sem, acc, False)
    @pl.loop(0, frames)
    def _(t):
        x = column_block(pieces, t)[1:-1].astype(F32)
        out = x + acc[pl.ds(pl.multiple_of(t * block, 8), block)].reshape(inner, rows, ch)
        if form == "wide":
            tile = tile_ref[0]
            col = lax.broadcasted_iota(jnp.int32, out.shape, 0)
            first = jnp.where(tile == 0, 1, 0)
            stop = jnp.where(tile == tile_ref[1] - 1, inner - 1, inner)
            outs[0][t] = jnp.where((col >= first) & (col < stop), out, 0.0).astype(BF16)
        else:
            write_block(out.astype(BF16), outs, t)


def run_fwd(form, out_cols, tile_info, pieces, gain, weight):
    frames, _, rows, ch = pieces[0].shape
    inner = sum(piece.shape[1] for piece in pieces) - 2
    return pl.pallas_call(
        functools.partial(fwd_kernel, form, len(pieces)),
        out_shape=[jax.ShapeDtypeStruct((frames, n, rows, ch), BF16) for n in out_cols],
        in_specs=[SM] + [VM] * (len(pieces) + 1) + [HB],
        out_specs=[VM] * len(out_cols),
        scratch_shapes=[
            pltpu.VMEM((6 * inner * rows, 9 * ch), BF16),
            pltpu.VMEM(weight.shape, BF16),
            pltpu.VMEM((frames * inner * rows, ch), F32),
            pltpu.SemaphoreType.DMA((PIECES,)),
        ],
        name=f"fwd_{form}",
        compiler_params=GRANT,
    )(tile_info, *pieces, gain, weight)


def bwd_kernel(form, n_x, n_g, *refs):
    tile_ref, *refs = refs
    xs, gs, (gain_ref, w_hbm, *rest) = refs[:n_x], refs[n_x : n_x + n_g], refs[n_x + n_g :]
    gf_ref, *outs, taps, w_buf, fac_ref, acc, sem = rest
    start_weights(w_hbm, w_buf, sem, True)
    frames, cols, rows, ch = gf_ref.shape
    block = cols * rows
    outer = cols + 2
    gain = gain_ref[...].astype(F32)
    low, high = edge_scales("odd" if form == "odd" else "even", tile_ref, F32)
    taps[4 * block : 6 * block, :] = jnp.zeros((2 * block, 9 * ch), BF16)

    def gradient(t):
        if form == "first":
            gc, lp, rp, from_l, from_r = gs
            mid = gc[t].astype(F32)
            left = from_l[t, :1].astype(F32) + lp[t, :1].astype(F32)
            right = from_r[t, 1:].astype(F32) + rp[t, 1:].astype(F32)
            return jnp.concatenate(
                [
                    left,
                    mid[:1] + from_l[t, 1:].astype(F32),
                    mid[1:-1],
                    mid[-1:] + from_r[t, :1].astype(F32),
                    right,
                ],
                axis=0,
            )
        return column_block(gs, t).astype(F32)

    def inputs(t):
        x = column_block(xs, t)
        return (x if n_x == 1 else x[1:-1]).astype(F32).reshape(block, ch)

    @pl.loop(0, frames)
    def _(t):
        g = gradient(t)
        if form != "odd":
            g = jnp.concatenate([g[:1] * low, g[1:-1], g[-1:] * high], axis=0)
        g = g.reshape(outer * rows, ch)
        before, after = row_shifts(g)
        for b, v in enumerate((after, g, before)):
            put_taps(taps, t, v, b, cols, ch, high if form == "odd" else None, True)
    @pl.loop(0, frames)
    def _(t):
        x = inputs(t)
        inv = lax.rsqrt(jnp.mean(x * x, axis=-1, keepdims=True) + EPS)
        u = x * inv * gain
        sig = jax.nn.sigmoid(u)
        fac_ref[t] = sig * (1.0 + u * (1.0 - sig)) * gain * inv
    convolve(taps, w_hbm, w_buf, sem, acc, True)
    for t in range(frames):
        x = inputs(t)
        inv2 = 1.0 / (jnp.mean(x * x, axis=-1, keepdims=True) + EPS)
        y = acc[t * block : (t + 1) * block] * fac_ref[t]
        dx = y - x * (inv2 * jnp.mean(y * x, axis=-1, keepdims=True))
        out = gradient(t)[1:-1] + dx.reshape(cols, rows, ch)
        gf_ref[t] = out
        if outs:
            write_block(out.astype(BF16), outs, t)


def run_bwd(form, out_cols, tile_info, xs, gs, gain, weight_back):
    frames, _, rows, ch = xs[0].shape
    cols = xs[0].shape[1] if len(xs) == 1 else sum(x.shape[1] for x in xs) - 2
    outs = [jax.ShapeDtypeStruct((frames, cols, rows, ch), F32)]
    outs += [jax.ShapeDtypeStruct((frames, n, rows, ch), BF16) for n in out_cols]
    return pl.pallas_call(
        functools.partial(bwd_kernel, form, len(xs), len(gs)),
        out_shape=outs,
        in_specs=[SM] + [VM] * (len(xs) + len(gs) + 1) + [HB],
        out_specs=[VM] * len(outs),
        scratch_shapes=[
            pltpu.VMEM((6 * cols * rows, 9 * ch), BF16),
            pltpu.VMEM(weight_back.shape, BF16),
            pltpu.VMEM((frames, cols * rows, ch), F32),
            pltpu.VMEM((frames * cols * rows, ch), F32),
            pltpu.SemaphoreType.DMA((PIECES,)),
        ],
        name=f"bwd_{form}",
        compiler_params=GRANT,
    )(tile_info, *xs, *gs, gain, weight_back)


def first_kernel(order_ref, latent_ref, x_ref, l_ref, r_ref):
    for t in range(x_ref.shape[0]):
        x = latent_ref[order_ref[t]]
        x_ref[t] = x
        l_ref[t] = x[:1]
        r_ref[t] = x[x.shape[0] - 1 :]


def run_first(order, latent):
    frames, cols, rows, ch = latent.shape
    return pl.pallas_call(
        first_kernel,
        out_shape=[jax.ShapeDtypeStruct((frames, n, rows, ch), BF16) for n in (cols, 1, 1)],
        in_specs=[SM, VM],
        out_specs=[VM] * 3,
        name="first",
        compiler_params=GRANT,
    )(order, latent)


def unwritten(*shapes, dtype=BF16):
    return tuple(
        pl.pallas_call(
            lambda out_ref: None,
            out_shape=jax.ShapeDtypeStruct(shape, dtype),
            out_specs=HB,
            name="unwritten",
        )()
        for shape in shapes
    )


def up_kernel(x_ref, wa_ref, wb_ref, spread_ref, *rest):
    pre_ref, *feat_refs, held, cells, phases, feats = rest
    frames, outer, rows, ch = x_ref.shape
    cols = outer - 2
    cu = wa_ref.shape[3]
    half = wa_ref.shape[0] * wa_ref.shape[2]
    block = outer * rows
    held[0 : 2 * block, :] = jnp.zeros((2 * block, 2 * half), BF16)
    for t in range(frames):
        held[(2 + t) * block : (3 + t) * block, :] = jnp.dot(
            x_ref[t].reshape(block, ch), spread_ref[...], preferred_element_type=F32
        ).astype(BF16)

    @pl.loop(0, 9)
    def _(tap):
        total = jnp.zeros((frames * block, cu), F32)
        for a in range(3):
            for part, w_ref in enumerate((wa_ref, wb_ref)):
                total = total + jnp.dot(
                    held[a * block : (a + frames) * block, part * half : (part + 1) * half],
                    w_ref[:, 9 * a + tap].reshape(half, cu),
                    preferred_element_type=F32,
                )
        cells[tap] = total

    shape = (frames, outer, rows, cu)
    by_phase = [[], []]
    for c in range(3):
        before, _ = row_shifts(cells[c])
        _, after = row_shifts(cells[6 + c])
        middle = cells[3 + c]
        by_phase[0].append((before + middle + cells[6 + c]).reshape(shape))
        by_phase[1].append((cells[c] + middle + after).reshape(shape))
    for p in range(2):
        left, mid, right = by_phase[p]
        phases[p, 0] = left[:, 0:cols] + mid[:, 1 : cols + 1] + right[:, 1 : cols + 1]
        phases[p, 1] = left[:, 1 : cols + 1] + mid[:, 1 : cols + 1] + right[:, 2 : cols + 2]

    @pl.loop(0, frames)
    def _(t):
        for w in range(cols):
            pair = [jnp.concatenate([phases[p, 0, t, w], phases[p, 1, t, w]], axis=1) for p in range(2)]
            lanes = slice(w * 2 * cu, (w + 1) * 2 * cu)
            for h in range(2):
                mine = slice(h * rows // 2, (h + 1) * rows // 2)
                piece = jnp.concatenate([pair[0][mine], pair[1][mine]], axis=0)
                pre_ref[2 * t + h, :, lanes] = piece
                feats[2 * t + h, :, lanes] = jax.nn.silu(piece).astype(BF16)

    for i, feat_ref in enumerate(feat_refs):
        feat_ref[...] = feats[i]


def run_up(x, wa, wb, spread):
    frames, outer, rows, ch = x.shape
    chunk = (rows, 2 * (outer - 2) * wa.shape[3])
    return pl.pallas_call(
        up_kernel,
        out_shape=[
            jax.ShapeDtypeStruct((2 * frames, *chunk), F32),
            *(jax.ShapeDtypeStruct(chunk, BF16) for _ in range(2 * frames)),
        ],
        in_specs=[VM] * 4,
        out_specs=[VM] * (1 + 2 * frames),
        scratch_shapes=[
            pltpu.VMEM((6 * outer * rows, spread.shape[1]), BF16),
            pltpu.VMEM((9, frames * outer * rows, wa.shape[3]), F32),
            pltpu.VMEM((2, 2, frames, outer - 2, rows, wa.shape[3]), F32),
            pltpu.VMEM((2 * frames, *chunk), BF16),
        ],
        name="up",
        compiler_params=GRANT,
    )(x, wa, wb, spread)


def exact_dot(value, ones, dims):
    total = None
    for _ in range(3):
        piece = value.astype(BF16)
        value = value - piece.astype(F32)
        part = lax.dot_general(piece, ones, dims, preferred_element_type=F32)
        total = part if total is None else total + part
    return total


GROUP = 48


def group_masks(rows, groups):
    row = lax.broadcasted_iota(jnp.int32, (rows, groups * GROUP), 0)
    lane = lax.broadcasted_iota(jnp.int32, (rows, groups * GROUP), 1)
    wanted = (row % 8) * 2 + (row // 8) % 2
    return lane // GROUP == wanted


def fold_matrix(groups):
    lane = lax.broadcasted_iota(jnp.int32, (groups * GROUP, GROUP), 0)
    column = lax.broadcasted_iota(jnp.int32, (groups * GROUP, GROUP), 1)
    return (lane % GROUP == column).astype(F32).astype(BF16)


def logit_kernel(half_ref, z_ref, w_hbm, out_ref, table, w_buf, sem):
    outs, keep = w_buf.shape
    span = z_ref.shape[1]
    groups = keep // span
    copy = pltpu.make_async_copy(
        w_hbm.at[:, pl.ds(pl.multiple_of(half_ref[0] * keep, 128), keep)], w_buf, sem
    )
    copy.start()
    mask = group_masks(z_ref.shape[0], groups)
    fold = fold_matrix(groups)
    copy.wait()

    @pl.loop(0, groups)
    def _(group):
        r, e = group // 2, group % 2
        true_row = 2 * (r % 4) + r // 4
        start = pl.multiple_of((2 * true_row + e) * span, 128)
        table[pl.ds(pl.multiple_of(group * GROUP, 16), GROUP), :] = jnp.concatenate(
            [w_buf[:, pl.ds(start, span)], jnp.zeros((GROUP - outs, span), BF16)], axis=0
        )

    pairs = lax.dot_general(
        z_ref[...], table[...], (((1,), (1,)), ((), ())), preferred_element_type=F32
    )
    pairs = jnp.where(mask, pairs, 0.0)
    patches = z_ref.shape[0] // groups
    summed = jnp.sum(pairs.reshape(patches, groups, groups * GROUP), axis=1)
    out_ref[...] = exact_dot(summed, fold, (((1,), (0,)), ((), ())))


def run_logit(half, z, weight, keep):
    outs = weight.shape[0]
    span = z.shape[1]
    groups = keep // span
    return pl.pallas_call(
        logit_kernel,
        out_shape=[
            jax.ShapeDtypeStruct((z.shape[0] // groups, GROUP), F32),
            jax.ShapeDtypeStruct((groups * GROUP, span), BF16),
        ],
        in_specs=[SM, VM, HB],
        out_specs=[VM, VM],
        scratch_shapes=[pltpu.VMEM((outs, keep), BF16), pltpu.SemaphoreType.DMA],
        name="logit",
        compiler_params=GRANT,
    )(half, z, weight)


def back_kernel(mine_ref, other_ref, coef_ref, table_ref, out_ref):
    groups = table_ref.shape[0] // GROUP
    patches = mine_ref.shape[0]
    squashed = jnp.tanh(mine_ref[...] + other_ref[...])
    grad = (coef_ref[...] * (1.0 - squashed * squashed)).astype(BF16)
    wide = lax.dot_general(
        grad, fold_matrix(groups), (((1,), (1,)), ((), ())), preferred_element_type=F32
    )
    wide = jnp.broadcast_to(wide[:, None, :], (patches, groups, groups * GROUP))
    wide = wide.reshape(patches * groups, groups * GROUP)
    wide = jnp.where(group_masks(patches * groups, groups), wide, 0.0).astype(BF16)
    out_ref[...] = jnp.dot(wide, table_ref[...], preferred_element_type=F32).astype(BF16)


def run_back(mine, other, coef, table):
    rows = mine.shape[0] * table.shape[0] // GROUP
    return pl.pallas_call(
        back_kernel,
        out_shape=jax.ShapeDtypeStruct((rows, table.shape[1]), BF16),
        in_specs=[VM] * 4,
        out_specs=VM,
        name="back",
        compiler_params=GRANT,
    )(mine, other, coef, table)


def sum_kernel(in_ref, out_ref):
    total = in_ref[0].astype(F32)
    for i in range(1, in_ref.shape[0]):
        total = total + in_ref[i].astype(F32)
    out_ref[...] = total.astype(BF16)


def run_sum(values):
    return pl.pallas_call(
        sum_kernel,
        out_shape=jax.ShapeDtypeStruct(values.shape[1:], BF16),
        in_specs=[VM],
        out_specs=VM,
        name="sum",
        compiler_params=GRANT,
    )(values)


def order_kernel(wa_ref, wb_ref, spread_ref, out_ref):
    half = wa_ref.shape[0] * wa_ref.shape[2]
    cu = wa_ref.shape[3]

    @pl.loop(0, wa_ref.shape[1])
    def _(tap):
        total = None
        for part, w_ref in enumerate((wa_ref, wb_ref)):
            turned = lax.dot_general(
                w_ref[:, tap].reshape(half, cu),
                spread_ref[:, part * half : (part + 1) * half],
                (((0,), (1,)), ((), ())),
                preferred_element_type=F32,
            )
            total = turned if total is None else total + turned
        out_ref[tap] = total.astype(BF16)


def run_order(wa, wb, spread):
    return pl.pallas_call(
        order_kernel,
        out_shape=jax.ShapeDtypeStruct((wa.shape[1], wa.shape[3], spread.shape[0]), BF16),
        in_specs=[VM] * 3,
        out_specs=VM,
        name="order",
        compiler_params=GRANT,
    )(wa, wb, spread)


def adj_kernel(pre_ref, w_ref, *rest):
    *grad_refs, gf_ref, l_ref, r_ref, held, acc_ref, grads = rest
    frames, cols, rows, ch = gf_ref.shape
    outer = cols + 2
    cu = w_ref.shape[1]
    block = outer * rows
    held[:, frames * block :, :] = jnp.zeros((9, 2 * block, cu), BF16)
    zero = jnp.zeros((1, rows, cu), F32)
    for i, grad_ref in enumerate(grad_refs):
        grads[i] = grad_ref[...]

    @pl.loop(0, frames)
    def _(t):
        chunks = []
        for h in range(2):
            pre = pre_ref[2 * t + h]
            sig = jax.nn.sigmoid(pre)
            grad = grads[2 * t + h].astype(F32) * sig * (1.0 + pre * (1.0 - sig))
            chunks.append(grad.astype(BF16).astype(F32))
        fine = []
        for p in range(2):
            low = slice(p * rows // 2, (p + 1) * rows // 2)
            whole = jnp.concatenate([chunks[0][low], chunks[1][low]], axis=0)
            even, odd = (
                jnp.concatenate(
                    [whole[:, (2 * w + q) * cu : (2 * w + q + 1) * cu][None] for w in range(cols)], axis=0
                )
                for q in range(2)
            )
            own = jnp.concatenate([zero, even + odd, zero], axis=0)
            later = jnp.concatenate([even[:1], odd[:-1] + even[1:], odd[-1:], zero], axis=0)
            sooner = jnp.concatenate([zero, even[:1], odd[:-1] + even[1:], odd[-1:]], axis=0)
            fine.append([v.reshape(block, cu) for v in (later, own, sooner)])
        for c in range(3):
            top, low = fine[0][c], fine[1][c]
            _, top_after = row_shifts(top)
            low_before, _ = row_shifts(low)
            for b, v in enumerate((low + top_after, top + low, low_before + top)):
                held[3 * b + c, pl.ds(pl.multiple_of(t * block, 16), block), :] = v.astype(BF16)
    acc_ref[...] = jnp.zeros_like(acc_ref)

    @pl.loop(0, 3)
    def _(a):
        total = acc_ref[...]
        for bc in range(9):
            total = total + jnp.dot(
                held[bc, pl.ds(pl.multiple_of((2 - a) * block, 16), frames * block), :],
                w_ref[9 * a + bc],
                preferred_element_type=F32,
            )
        acc_ref[...] = total

    out = acc_ref[...]
    out = out.reshape(frames, outer, rows, ch)
    gf_ref[...] = out[:, 1:-1]
    l_ref[...] = out[:, :2].astype(BF16)
    r_ref[...] = out[:, -2:].astype(BF16)


def run_adj(grads, pre, weight, frames, cols):
    rows = pre.shape[1]
    cu, ch = weight.shape[1:]
    return pl.pallas_call(
        adj_kernel,
        out_shape=[
            jax.ShapeDtypeStruct((frames, cols, rows, ch), F32),
            jax.ShapeDtypeStruct((frames, 2, rows, ch), BF16),
            jax.ShapeDtypeStruct((frames, 2, rows, ch), BF16),
        ],
        in_specs=[VM] * (2 + len(grads)),
        out_specs=[VM] * 3,
        scratch_shapes=[
            pltpu.VMEM((9, 6 * (cols + 2) * rows, cu), BF16),
            pltpu.VMEM((frames * (cols + 2) * rows, ch), F32),
            pltpu.VMEM(pre.shape, BF16),
        ],
        name="adj",
        compiler_params=GRANT,
    )(pre, weight, *grads)


def on_device(latent, frame_order, section_weight, section_gain, up_weight, reward_weight, reward_coef):
    segs = lax.axis_size("segment")
    chips = lax.axis_size("chip")
    tiles = 2 * chips
    seg = lax.axis_index("segment")
    core = lax.axis_index("core")
    tile = 2 * lax.axis_index("chip") + core
    frames, rows, cols, ch = latent.shape
    cu = up_weight.shape[2]
    outs_dev = reward_coef.shape[0]
    last = segs - 1
    halves = segs // frames
    span = 2 * cols * cu
    keep = 2 * rows // halves * 2 * span
    barrier = lax.optimization_barrier
    tile_info = jnp.stack([tile, jnp.full_like(tile, tiles)])
    block = (frames, cols, rows, ch)
    side = (frames, 1, rows, ch)
    side2 = (frames, 2, rows, ch)

    def route(pairs_of_segments, shift):
        return [
            (source * tiles + t, target * tiles + t + shift)
            for source, target in pairs_of_segments
            for t in range(tiles)
            if 0 <= t + shift < tiles
        ]

    def send(value, source, target):
        return lax.ppermute(value, AXES, route([(source, target)], 0))

    def beside(value, shift):
        return lax.ppermute(value, AXES, route([(s, s) for s in range(segs)], shift))

    def hop_route(source, target, shift):
        step = target - source
        pairs = [(s, s + step) for s in range(source % 2, segs, 2) if 0 <= s + step < segs]
        return pairs, shift

    def hop(center, left, right, source, target):
        center, left, right = (
            lax.ppermute(value, AXES, route(*hop_route(source, target, shift)))
            for value, shift in ((center, 0), (right, 1), (left, -1))
        )
        return left, center, right

    def turn_round(pairs_of_segments, shift):
        return [
            (source * tiles + t, target * tiles + (t + shift) % tiles)
            for source, target in pairs_of_segments
            for t in range(tiles)
        ]

    def half_hop(first_three, last_three, source, target):
        to_left, to_right = (-1, 0) if source % 2 == 0 else (0, 1)
        left = lax.ppermute(last_three, AXES, turn_round(*hop_route(source, target, to_right)))
        right = lax.ppermute(first_three, AXES, turn_round(*hop_route(source, target, to_left)))
        return left, right

    def gather_up():
        own = up_weight.shape[1]
        source = jnp.pad(up_weight, ((0, 0), (0, PAD - own), (0, 0)))
        wa = lax.all_to_all(
            jnp.broadcast_to(source[None], (chips, *source.shape)), "chip", 0, 0, tiled=True
        )
        wb = lax.ppermute(wa, "core", [(0, 1), (1, 0)])
        channel = lax.broadcasted_iota(jnp.int32, (ch, tiles * PAD), 0)
        place = lax.broadcasted_iota(jnp.int32, (ch, tiles * PAD), 1)
        other, chip_of, within = place // (chips * PAD), place // PAD % chips, place % PAD
        origin = 2 * chip_of + jnp.where(other == 0, core, 1 - core)
        spread = ((within < own) & (channel == origin * own + within)).astype(BF16)
        return wa, wb, spread, run_order(wa, wb, spread)

    up_shape = (chips, 27, PAD, cu)

    def turn(weight):
        return weight[0].transpose(0, 2, 1).reshape(27 * ch, ch)

    def start():
        x, left, right = run_first(frame_order, latent.transpose(0, 2, 1, 3))
        return beside(right, 1), x, beside(left, -1)

    weight_fwd = section_weight[0].reshape(27 * ch, ch)
    gathered = lax.cond(
        seg == last,
        gather_up,
        lambda: unwritten(up_shape, up_shape, (ch, tiles * PAD), (27, cu, ch)),
    )
    turned = lax.cond(seg > 1, lambda: turn(section_weight), lambda: unwritten((27 * ch, ch))[0])
    state = lax.cond(seg == 0, start, lambda: unwritten(side, block, side))
    gathered, turned, state = barrier((gathered, turned, state))

    three = (frames, 3, rows, ch)
    taken = [state]
    for k in range(last):
        wide = k == last - 1
        made_shapes = (block, side2, side2) if wide else (three, three)

        def go(state=state, k=k, wide=wide, made_shapes=made_shapes):
            form = "odd" if k % 2 else "even"
            made = lax.cond(
                seg == k,
                lambda: tuple(
                    run_fwd(form, [m[1] for m in made_shapes], tile_info, state, section_gain, weight_fwd)
                ),
                lambda: unwritten(*made_shapes),
            )
            return hop(*made, k, k + 1) if wide else half_hop(*made, k, k + 1)

        given = (side2, block, side2) if wide else (three, three)
        state = lax.cond(
            (seg == k) | (seg == k + 1), go, lambda given=given: unwritten(*given)
        )
        taken.append(state)
        if k == 1:
            late, state = barrier((section_weight, state))
            turned_late = lax.cond(
                seg <= 1, lambda late=late: turn(late), lambda: unwritten((27 * ch, ch))[0]
            )
            turned_late, state = barrier((turned_late, state))
            taken[-1] = state

    chunk = (rows, span)

    def upsampled():
        (deep,) = run_fwd("wide", [cols + 2], tile_info, state, section_gain, weight_fwd)
        return tuple(run_up(deep, *gathered[:3]))

    pre, *feats = lax.cond(
        seg == last,
        upsampled,
        lambda: (
            unwritten((segs, *chunk), dtype=F32)[0],
            *unwritten(*([chunk] * last)),
            jnp.zeros(chunk, BF16),
        ),
    )
    mine = functools.reduce(jnp.add, [send(feats[k], last, k) for k in range(last)], feats[last])
    coef = jnp.pad(reward_coef, (0, GROUP - outs_dev))[None]
    mine, coef = barrier((mine, coef))
    everyone = lax.cond(
        seg >= 0,
        lambda: lax.all_to_all(
            jnp.broadcast_to(mine[None], (tiles, *chunk)), TILE, 0, 0, tiled=True
        ),
        lambda: unwritten((tiles, *chunk))[0],
    )
    half = (seg % halves).reshape(1)
    partial, table = run_logit(half, everyone.reshape(tiles * rows, span), reward_weight.T, keep)
    group = [(s, s // halves * halves + (s + 1) % halves) for s in range(segs)]
    other = lax.ppermute(partial, "segment", group)
    shares = run_back(partial, other, coef, table)
    shares = lax.all_to_all(shares.reshape(tiles, *chunk), TILE, 0, 0, tiled=True)
    share = run_sum(shares)
    grads = [send(share, k, last) for k in range(last)] + [share]

    results = {}
    for k in range(last, 0, -1):

        def go_back(state=state, k=k):
            def live():
                if k == last:
                    deep, lp, rp = run_adj(grads, pre, gathered[3], frames, cols)
                    from_r, from_l = beside(lp, -1), beside(rp, 1)
                    gs = (deep, lp, rp, from_l, from_r)
                    made = run_bwd(
                        "first", (cols, 1, 1), tile_info, taken[k][1:2], gs, section_gain, turned
                    )
                else:
                    form = "odd" if k % 2 else "even"
                    weight = turned if k > 1 else turned_late
                    made = run_bwd(form, (3, 3), tile_info, taken[k], state, section_gain, weight)
                return (*made[1:], made[0])

            shapes = (block, side, side) if k == last else (three, three)
            *made, result = lax.cond(
                seg == k,
                live,
                lambda: (*unwritten(*shapes), *unwritten(block, dtype=F32)),
            )
            passed = hop(*made, k, k - 1) if k == last else half_hop(*made, k, k - 1)
            return passed, result

        given = (side, block, side) if k == last else (three, three)
        state, results[k] = lax.cond(
            (seg == k) | (seg == k - 1),
            go_back,
            lambda given=given: (unwritten(*given), unwritten(block, dtype=F32)[0]),
        )

    def finish(k):
        if k == 0:
            result = run_bwd(
                "even", (), tile_info, taken[0][1:2], state, section_gain, turned_late
            )[0]
        else:
            result = results[k]
            if k != last and k % 2:
                moved = turn_round([(s, s) for s in range(segs)], 1)
                left = lax.ppermute(result[:, cols - 2 :], AXES, moved)
                result = jnp.concatenate([left, result[:, : cols - 2]], axis=1)
        return result.transpose(0, 2, 1, 3)

    return lax.switch(seg, [functools.partial(finish, k) for k in range(segs)])[None]


def solution(mesh):
    shape = mesh.devices.shape
    fine = jax.sharding.Mesh(mesh.devices.reshape(shape[0], shape[1] // 2, 2), AXES)
    in_specs = (
        P(None, None, TILE, None),
        P(),
        P("segment", None, None, None),
        P("segment", None),
        P(None, TILE, None),
        P(None, TILE),
        P(TILE),
    )
    out_specs = P("segment", None, None, TILE, None)
    return jax.shard_map(
        on_device, mesh=fine, in_specs=in_specs, out_specs=out_specs, check_vma=False
    )
```

profile of v0, /device:TPU:2, one launch (start us, length us, event | category | flops | bytes accessed | tf_op | source)
XLA Modules:
  0.0 291.9 jit_solution(17204459662557609314)
XLA Ops:
  0.0 0.9 copy-done.3
  0.9 9.8 %conditional.37 = (bf16[4,1,8,384]{3,2,1,0:T(8,128)(2,1)}, bf16[4,4,8,384]{3,2,1,0:T(8,128)(2,1)S(1)}, bf16[4,1,8,384]{3,2,1,0:T(8,128)(2,1)}) conditional(s32[]{:T(128)} %convert_element_type.95, () %tuple.360, (bf16[4,8,4,384]{3,2,1,0:T(4,128)(2,1)S(1)}, s32[4]{0:T(128)S(1)}) %tuple.542), branch_computations={%region_4.5_spmd, %region_5.6_spmd} | conditional | bytes 393320 | solution.py:668
  0.9 0.6 first.1
  1.5 1.9 collective-permute-start.33
  3.4 5.8 %collective-permute-start.34 = (bf16[4,1,8,384]{3,2,1,0:T(8,128)(2,1)S(1)}, bf16[4,1,8,384]{3,2,1,0:T(8,128)(2,1)}, u32[]{:S(2)}, u32[]{:S(2)}) collective-permute-start(bf16[4,1,8,384]{3,2,1,0:T(8,128)(2,1)S(1)} %get-tuple-element.493), channel_id=1, source_target_pairs={{1,0},{2,1},{3,2},{4,3},{5,4},{6,5},{7,6},{8,7},{9,8},{10,9},{11,1... | collective-permute-start | bytes 73736 | tf_op jit(solution)/shard_map/cond/branch_1_fun/ppermute | solution.py:611
  9.2 1.5 collective-permute-done.34
  10.7 0.1 pad_add_fusion
  10.8 0.6 copy-done.1
  11.4 9.9 %conditional.38 = (bf16[4,3,8,384]{3,2,1,0:T(8,128)(2,1)}, bf16[4,3,8,384]{3,2,1,0:T(8,128)(2,1)}) conditional(s32[]{:T(128)} %convert_element_type.96, () %tuple.364, (s32[]{:T(128)}, s32[2]{0:T(128)S(1)}, bf16[4,1,8,384]{3,2,1,0:T(8,128)(2,1)}, bf16[4,4,8,384]{3,2,1,0:T(8,128)(2,1)S(1)}, bf16[4,1,8,384]{3,2,1,0:T(8,128)(2,1)}, ...), branch_computations={%region_6.7_spmd, %region_7.10_spmd} | conditional | flops 2 | bytes 590006 | solution.py:689
  11.4 4.7 %conditional = ((bf16[4,3,8,384]{3,2,1,0:T(8,128)(2,1)S(1)}, bf16[4,3,8,384]{3,2,1,0:T(8,128)(2,1)S(1)})) conditional(s32[]{:T(128)} %convert_element_type.24, () %tuple.239, (s32[2]{0:T(128)S(1)}, bf16[4,1,8,384]{3,2,1,0:T(8,128)(2,1)}, bf16[4,4,8,384]{3,2,1,0:T(8,128)(2,1)S(1)}, bf16[4,1,8,384]{3,2,1,0:T(8,128)(2,1)}, bf16[1,384]{1,0:T(2,128)(2,1)S(1)}, ...), branch_computations={%region_8.8_spmd, %region_9.9_spmd} | conditional | bytes 24 | solution.py:679
  11.4 4.7 %fwd_even.4 = (bf16[4,3,8,384]{3,2,1,0:T(8,128)(2,1)S(1)}, bf16[4,3,8,384]{3,2,1,0:T(8,128)(2,1)S(1)}) custom-call(s32[2]{0:T(128)S(1)} %get-tuple-element.494.refs_0_, bf16[4,1,8,384]{3,2,1,0:T(8,128)(2,1)} %get-tuple-element.495.refs_1_, bf16[4,4,8,384]{3,2,1,0:T(8,128)(2,1)S(1)} %get-tuple-element.496.refs_2_, ...), custom_call_target="tpu_custom_call" | custom-call | tf_op jit(solution)/shard_map/cond/branch_1_fun/cond/branch_1_fun/fwd_even/pallas_call | solution.py:144
  16.1 1.9 collective-permute-start
  18.0 1.9 collective-permute-start.1
  19.9 1.4 collective-permute-done.1
  21.2 11.5 %conditional.40 = (bf16[10368,384]{1,0:T(8,128)(2,1)}) conditional(s32[]{:T(128)} %convert_element_type.98, () %tuple.367, bf16[1,27,384,384]{3,2,1,0:T(8,128)(2,1)} %param.85), branch_computations={%region_14.15_spmd, %region_15.16_spmd} | conditional | bytes 15925256 | solution.py:695
  21.2 11.5 %copy.20 = bf16[27,384,384]{2,1,0:T(8,128)(2,1)} copy(bf16[27,384,384]{1,2,0:T(8,128)(2,1)} %bitcast.60) | data formatting | bytes 15925248 | tf_op jit(solution)/shard_map/cond/branch_1_fun/transpose | solution.py:655
  32.9 0.1 conditional.46
  33.0 1.3 collective-permute-start.38
  34.3 0.7 collective-permute-start.39
  35.0 0.7 collective-permute-start.40
  35.7 0.7 collective-permute-start.41
  36.3 0.7 collective-permute-start.42
  37.0 78.7 %collective-permute-done.38 = bf16[8,1536]{1,0:T(8,128)(2,1)S(1)} collective-permute-done((bf16[8,1536]{1,0:T(8,128)(2,1)S(1)}, bf16[8,1536]{1,0:T(8,128)(2,1)S(1)}, u32[]{:S(2)}, u32[]{:S(2)}) %collective-permute-start.38) | collective-permute-done | bytes 24608 | tf_op jit(solution)/shard_map/ppermute | solution.py:608
  115.7 0.7 collective-permute-start.43
  116.3 0.8 collective-permute-start.44
  117.3 17.9 %conditional.47 = (bf16[256,1536]{1,0:T(8,128)(2,1)S(1)}) conditional(s32[]{:T(128)} %convert_element_type.104, () %tuple.389, bf16[8,1536]{1,0:T(8,128)(2,1)S(1)} %add_add_fusion), branch_computations={%region_38.39_spmd, %region_39.40_spmd} | conditional | bytes 2383880 | solution.py:719
  117.4 17.8 %all_to_all.14 = bf16[32,8,1536]{2,1,0:T(8,128)(2,1)S(1)} all-to-all(bf16[32,8,1536]{2,1,0:T(8,128)(2,1)S(1)} %broadcast_in_dim.38), channel_id=1, replica_groups=mesh['segment'=8,'chip'=16,'core'=2] {'chip','core'}, dimensions={0} | all-to-all | bytes 1572864 | tf_op jit(solution)/shard_map/cond/branch_1_fun/all_to_all | solution.py:721
  135.2 2.1 copy-done
  137.3 2.0 logit.1
  139.3 2.2 collective-permute-start.45
  141.5 1.6 collective-permute-done.45.other_ref
  143.1 1.1 back.1
  144.2 17.8 %all_to_all.15.in_ref = bf16[32,8,1536]{2,1,0:T(8,128)(2,1)S(1)} all-to-all(bf16[32,8,1536]{2,1,0:T(8,128)(2,1)S(1)} %bitcast.48), channel_id=1, replica_groups=mesh['segment'=8,'chip'=16,'core'=2] {'chip','core'}, dimensions={0} | all-to-all | bytes 1572864 | tf_op jit(solution)/shard_map/all_to_all | solution.py:731
  162.0 0.1 sum.1
  162.1 8.1 %collective-permute-start.46 = (bf16[8,1536]{1,0:T(8,128)(2,1)S(1)}, bf16[8,1536]{1,0:T(8,128)(2,1)S(1)}, u32[]{:S(2)}, u32[]{:S(2)}) collective-permute-start(bf16[8,1536]{1,0:T(8,128)(2,1)S(1)} %sum.1), channel_id=1, source_target_pairs={{0,224},{1,225},{2,226},{3,227},{4,228},{5,229},{6,230},{7,231},{8... | collective-permute-start | bytes 73736 | tf_op jit(solution)/shard_map/ppermute | solution.py:608
  170.2 0.7 collective-permute-start.47
  170.9 0.7 collective-permute-start.48
  171.5 0.7 collective-permute-start.49
  172.2 0.7 collective-permute-start.50
  172.9 0.7 collective-permute-start.51
  173.6 0.7 collective-permute-start.52
  174.6 111.6 %conditional.54 = (bf16[4,3,8,384]{3,2,1,0:T(8,128)(2,1)}, bf16[4,3,8,384]{3,2,1,0:T(8,128)(2,1)}, f32[4,4,8,384]{3,2,1,0:T(8,128)}) conditional(s32[]{:T(128)} %convert_element_type.96, () %tuple.363, (s32[]{:T(128)}, s32[2]{0:T(128)S(1)}, bf16[4,3,8,384]{3,2,1,0:T(8,128)(2,1)}, bf16[4,3,8,384]{3,2,1,0:T(8,128)(2,1)}, ...), branch_computations={%region_64.65_spmd, %region_65.68_spmd} | conditional | flops 2 | bytes 590022 | solution.py:763
  174.7 1.3 collective-permute-start.30
  176.0 1.3 collective-permute-start.31
  177.3 108.9 %collective-permute-done.30 = bf16[4,3,8,384]{3,2,1,0:T(8,128)(2,1)} collective-permute-done((bf16[4,3,8,384]{3,2,1,0:T(8,128)(2,1)S(1)}, bf16[4,3,8,384]{3,2,1,0:T(8,128)(2,1)}, u32[]{:S(2)}, u32[]{:S(2)}) %collective-permute-start.30) | collective-permute-done | bytes 73760 | tf_op jit(solution)/shard_map/cond/branch_1_fun/ppermute | solution.py:634
  286.2 5.0 %conditional.55 = (f32[1,4,8,4,384]{4,3,2,1,0:T(4,128)S(1)}) conditional(s32[]{:T(128)} %clamp.3, (s32[2]{0:T(128)S(1)}, bf16[4,4,8,384]{3,2,1,0:T(8,128)(2,1)S(1)}, bf16[4,3,8,384]{3,2,1,0:T(8,128)(2,1)}, bf16[4,3,8,384]{3,2,1,0:T(8,128)(2,1)}, bf16[1,384]{1,0:T(2,128)(2,1)S(1)}, ...), branch_computations={%region_68.69_spmd, %region_69.70_spmd, %region_70.71_spmd, %regio... | conditional | flops 49152 | bytes 1572912 | solution.py:782
  286.2 4.9 %bwd_even.7 = f32[4,4,8,384]{3,2,1,0:T(8,128)S(1)} custom-call(s32[2]{0:T(128)S(1)} %get-tuple-element.765.refs_0_, bf16[4,4,8,384]{3,2,1,0:T(8,128)(2,1)S(1)} %get-tuple-element.766.refs_1_, bf16[4,3,8,384]{3,2,1,0:T(8,128)(2,1)} %get-tuple-element.767.refs_2_, bf16[4,3,8,384]{3,2,1,0:T(8,128)(2,1)} %get-tuple-element.768.refs_3_, ...), custom_call_target="tpu_custom_call" | custom-call | tf_op jit(solution)/shard_map/cond/branch_0_fun/bwd_even/pallas_call | solution.py:227
  291.2 0.7 copy-done.2
  (93 shorter events, 0.7 us)
Async XLA Ops:
  0.0 0.9 copy-start.3
  0.0 0.9 copy-start.4
  1.5 7.7 %collective-permute-start.33 = (bf16[4,1,8,384]{3,2,1,0:T(8,128)(2,1)S(1)}, bf16[4,1,8,384]{3,2,1,0:T(8,128)(2,1)}, u32[]{:S(2)}, u32[]{:S(2)}) collective-permute-start(bf16[4,1,8,384]{3,2,1,0:T(8,128)(2,1)S(1)} %get-tuple-element.491), channel_id=1, source_target_pairs={{0,1},{1,2},{2,3},{3,4},{4,5},{5,6},{6,7},{7,8},{8,9},{9,10},{10,1... | collective-permute-start | bytes 73736 | tf_op jit(solution)/shard_map/cond/branch_1_fun/ppermute | solution.py:611
  3.4 7.3 %collective-permute-start.34 = (bf16[4,1,8,384]{3,2,1,0:T(8,128)(2,1)S(1)}, bf16[4,1,8,384]{3,2,1,0:T(8,128)(2,1)}, u32[]{:S(2)}, u32[]{:S(2)}) collective-permute-start(bf16[4,1,8,384]{3,2,1,0:T(8,128)(2,1)S(1)} %get-tuple-element.493), channel_id=1, source_target_pairs={{1,0},{2,1},{3,2},{4,3},{5,4},{6,5},{7,6},{8,7},{9,8},{10,9},{11,1... | collective-permute-start | bytes 73736 | tf_op jit(solution)/shard_map/cond/branch_1_fun/ppermute | solution.py:611
  10.7 0.7 copy-start.1
  16.1 3.8 %collective-permute-start = (bf16[4,3,8,384]{3,2,1,0:T(8,128)(2,1)S(1)}, bf16[4,3,8,384]{3,2,1,0:T(8,128)(2,1)}, u32[]{:S(2)}, u32[]{:S(2)}) collective-permute-start(bf16[4,3,8,384]{3,2,1,0:T(8,128)(2,1)S(1)} %get-tuple-element.507), channel_id=1, source_target_pairs={{0,32},{1,33},{2,34},{3,35},{4,36},{5,37},{6,38},{7,39},{8,40},{9,... | collective-permute-start | bytes 221192 | tf_op jit(solution)/shard_map/cond/branch_1_fun/ppermute | solution.py:634
  18.0 3.3 %collective-permute-start.1 = (bf16[4,3,8,384]{3,2,1,0:T(8,128)(2,1)S(1)}, bf16[4,3,8,384]{3,2,1,0:T(8,128)(2,1)}, u32[]{:S(2)}, u32[]{:S(2)}) collective-permute-start(bf16[4,3,8,384]{3,2,1,0:T(8,128)(2,1)S(1)} %get-tuple-element.508), channel_id=1, source_target_pairs={{0,63},{1,32},{2,33},{3,34},{4,35},{5,36},{6,37},{7,38},{8,39},{9,... | collective-permute-start | bytes 221192 | tf_op jit(solution)/shard_map/cond/branch_1_fun/ppermute | solution.py:635
  32.9 84.3 %copy-start.5 = (f32[40]{0:T(128)S(1)}, f32[40]{0:T(128)}, u32[]{:S(2)}) copy-start(f32[40]{0:T(128)} %param.89) | copy-start | bytes 484
  33.0 82.7 %collective-permute-start.38 = (bf16[8,1536]{1,0:T(8,128)(2,1)S(1)}, bf16[8,1536]{1,0:T(8,128)(2,1)S(1)}, u32[]{:S(2)}, u32[]{:S(2)}) collective-permute-start(bf16[8,1536]{1,0:T(8,128)(2,1)S(1)} %get-tuple-element.878), channel_id=1, source_target_pairs={{224,0},{225,1},{226,2},{227,3},{228,4},{229,5},{230,6},{231,7},{2... | collective-permute-start | bytes 73736 | tf_op jit(solution)/shard_map/ppermute | solution.py:608
  34.3 82.0 %collective-permute-start.39 = (bf16[8,1536]{1,0:T(8,128)(2,1)S(1)}, bf16[8,1536]{1,0:T(8,128)(2,1)S(1)}, u32[]{:S(2)}, u32[]{:S(2)}) collective-permute-start(bf16[8,1536]{1,0:T(8,128)(2,1)S(1)} %get-tuple-element.879), channel_id=1, source_target_pairs={{224,32},{225,33},{226,34},{227,35},{228,36},{229,37},{230,38},{23... | collective-permute-start | bytes 73736 | tf_op jit(solution)/shard_map/ppermute | solution.py:608
  35.0 82.2 %collective-permute-start.40 = (bf16[8,1536]{1,0:T(8,128)(2,1)S(1)}, bf16[8,1536]{1,0:T(8,128)(2,1)S(1)}, u32[]{:S(2)}, u32[]{:S(2)}) collective-permute-start(bf16[8,1536]{1,0:T(8,128)(2,1)S(1)} %get-tuple-element.880), channel_id=1, source_target_pairs={{224,64},{225,65},{226,66},{227,67},{228,68},{229,69},{230,70},{23... | collective-permute-start | bytes 73736 | tf_op jit(solution)/shard_map/ppermute | solution.py:608
  35.7 81.6 %collective-permute-start.41 = (bf16[8,1536]{1,0:T(8,128)(2,1)S(1)}, bf16[8,1536]{1,0:T(8,128)(2,1)S(1)}, u32[]{:S(2)}, u32[]{:S(2)}) collective-permute-start(bf16[8,1536]{1,0:T(8,128)(2,1)S(1)} %get-tuple-element.881), channel_id=1, source_target_pairs={{224,96},{225,97},{226,98},{227,99},{228,100},{229,101},{230,102},... | collective-permute-start | bytes 73736 | tf_op jit(solution)/shard_map/ppermute | solution.py:608
  36.3 80.9 %collective-permute-start.42 = (bf16[8,1536]{1,0:T(8,128)(2,1)S(1)}, bf16[8,1536]{1,0:T(8,128)(2,1)S(1)}, u32[]{:S(2)}, u32[]{:S(2)}) collective-permute-start(bf16[8,1536]{1,0:T(8,128)(2,1)S(1)} %get-tuple-element.882), channel_id=1, source_target_pairs={{224,128},{225,129},{226,130},{227,131},{228,132},{229,133},{230,1... | collective-permute-start | bytes 73736 | tf_op jit(solution)/shard_map/ppermute | solution.py:608
  115.7 1.6 collective-permute-start.43
  116.3 0.9 collective-permute-start.44
  135.2 2.1 copy-start
  139.3 3.8 %collective-permute-start.45 = (f32[16,48]{1,0:T(8,128)S(1)}, f32[16,48]{1,0:T(8,128)S(1)}, u32[]{:S(2)}, u32[]{:S(2)}) collective-permute-start(f32[16,48]{1,0:T(8,128)S(1)} %get-tuple-element.886.mine_ref), channel_id=1, source_target_pairs={{0,32},{32,0},{64,96},{96,64},{128,160},{160,128},{192,224},{224,1... | collective-permute-start | bytes 9224 | tf_op jit(solution)/shard_map/ppermute | solution.py:729
  162.1 10.8 %collective-permute-start.46 = (bf16[8,1536]{1,0:T(8,128)(2,1)S(1)}, bf16[8,1536]{1,0:T(8,128)(2,1)S(1)}, u32[]{:S(2)}, u32[]{:S(2)}) collective-permute-start(bf16[8,1536]{1,0:T(8,128)(2,1)S(1)} %sum.1), channel_id=1, source_target_pairs={{0,224},{1,225},{2,226},{3,227},{4,228},{5,229},{6,230},{7,231},{8... | collective-permute-start | bytes 73736 | tf_op jit(solution)/shard_map/ppermute | solution.py:608
  170.2 3.4 %collective-permute-start.47 = (bf16[8,1536]{1,0:T(8,128)(2,1)S(1)}, bf16[8,1536]{1,0:T(8,128)(2,1)S(1)}, u32[]{:S(2)}, u32[]{:S(2)}) collective-permute-start(bf16[8,1536]{1,0:T(8,128)(2,1)S(1)} %sum.1), channel_id=1, source_target_pairs={{32,224},{33,225},{34,226},{35,227},{36,228},{37,229},{38,230},{39... | collective-permute-start | bytes 73736 | tf_op jit(solution)/shard_map/ppermute | solution.py:608
  170.9 3.4 %collective-permute-start.48 = (bf16[8,1536]{1,0:T(8,128)(2,1)S(1)}, bf16[8,1536]{1,0:T(8,128)(2,1)S(1)}, u32[]{:S(2)}, u32[]{:S(2)}) collective-permute-start(bf16[8,1536]{1,0:T(8,128)(2,1)S(1)} %sum.1), channel_id=1, source_target_pairs={{64,224},{65,225},{66,226},{67,227},{68,228},{69,229},{70,230},{71... | collective-permute-start | bytes 73736 | tf_op jit(solution)/shard_map/ppermute | solution.py:608
  171.5 2.7 collective-permute-start.49
  172.2 2.1 collective-permute-start.50
  172.9 1.4 collective-permute-start.51
  173.6 0.7 collective-permute-start.52
  174.7 111.5 %collective-permute-start.30 = (bf16[4,3,8,384]{3,2,1,0:T(8,128)(2,1)S(1)}, bf16[4,3,8,384]{3,2,1,0:T(8,128)(2,1)}, u32[]{:S(2)}, u32[]{:S(2)}) collective-permute-start(bf16[4,3,8,384]{3,2,1,0:T(8,128)(2,1)S(1)} %get-tuple-element.762), channel_id=1, source_target_pairs={{32,1},{33,2},{34,3},{35,4},{36,5},{37,6},{38,7},{39,8},{40,9},{41... | collective-permute-start | bytes 221192 | tf_op jit(solution)/shard_map/cond/branch_1_fun/ppermute | solution.py:634
  176.0 110.2 %collective-permute-start.31 = (bf16[4,3,8,384]{3,2,1,0:T(8,128)(2,1)S(1)}, bf16[4,3,8,384]{3,2,1,0:T(8,128)(2,1)}, u32[]{:S(2)}, u32[]{:S(2)}) collective-permute-start(bf16[4,3,8,384]{3,2,1,0:T(8,128)(2,1)S(1)} %get-tuple-element.763), channel_id=1, source_target_pairs={{32,0},{33,1},{34,2},{35,3},{36,4},{37,5},{38,6},{39,7},{40,8},{41... | collective-permute-start | bytes 221192 | tf_op jit(solution)/shard_map/cond/branch_1_fun/ppermute | solution.py:635
  291.2 0.7 copy-start.2
where the time goes:
time: 293 us; the launch traced here: 292 us
  waiting for transfers between devices  192 us (66%)
  blocking collectives  35.6 us (12%)
  starting transfers between devices  33.7 us (12%)
  local copies, waits for them, and re-layouts  15.9 us (5%)
  Pallas kernels  13.4 us (5%)
    ppermute x2, waiting for transfers between devices, half_hop(): lax.ppermute(last_three, AXES, turn_round(*hop_route(source, target, to_r...  109 us
    ppermute x14, waiting for transfers between devices, send(): return lax.ppermute(value, AXES, route([(source, target)], 0))  78.7 us
    all_to_all x1, blocking collectives, on_device(): lax.all_to_all(shares.reshape(tiles, *chunk), TILE, 0, 0, tiled=True)  17.8 us
    all_to_all x1, blocking collectives, on_device(): lax.all_to_all(jnp.broadcast_to(mine[None], (tiles, *chunk)), TILE, 0, 0,...  17.8 us
    ppermute x14, starting transfers between devices, send(): return lax.ppermute(value, AXES, route([(source, target)], 0))  17.5 us
    transpose x1, local copies, waits for them, and re-layouts, turn(): return weight[0].transpose(0, 2, 1).reshape(27 * ch, ch)  11.5 us
    ppermute x2, starting transfers between devices, beside(): lax.ppermute(value, AXES, route([(s, s) for s in range(segs)], shift))  7.67 us
  transfers between devices with their start and end apart: 21, of which 5 were waited for; matrix products, arithmetic and copies ran while one was open for 0% of the time, Pallas kernels for 0%

commit v1 on v0

--- a/solution.py
+++ b/solution.py
@@ -241,6 +241,33 @@
     )(tile_info, *xs, *gs, gain, weight_back)
 
 
+def turn_kernel(in_ref, out_ref):
+    size = in_ref.shape[1]
+    row = lax.broadcasted_iota(jnp.int32, (size, size), 0)
+    lane = lax.broadcasted_iota(jnp.int32, (size, size), 1)
+    same = (row == lane).astype(F32).astype(BF16)
+
+    @pl.loop(0, in_ref.shape[0])
+    def _(i):
+        out_ref[i] = lax.dot_general(
+            same, in_ref[i], (((1,), (1,)), ((), ())), preferred_element_type=F32
+        ).astype(BF16)
+
+
+def run_turn(weight):
+    taps, ch, _ = weight.shape
+    spec = pl.BlockSpec((3, ch, ch), lambda i: (i, 0, 0))
+    return pl.pallas_call(
+        turn_kernel,
+        out_shape=jax.ShapeDtypeStruct(weight.shape, BF16),
+        grid=(taps // 3,),
+        in_specs=[spec],
+        out_specs=spec,
+        name="turn",
+        compiler_params=GRANT,
+    )(weight).reshape(taps * ch, ch)
+
+
 def first_kernel(order_ref, latent_ref, x_ref, l_ref, r_ref):
     for t in range(x_ref.shape[0]):
         x = latent_ref[order_ref[t]]
@@ -414,7 +441,7 @@
             jax.ShapeDtypeStruct((z.shape[0] // groups, GROUP), F32),
             jax.ShapeDtypeStruct((groups * GROUP, span), BF16),
         ],
-        in_specs=[SM, VM, HB],
+        in_specs=[SM, VM, pl.BlockSpec(memory_space=pltpu.HBM)],
         out_specs=[VM, VM],
         scratch_shapes=[pltpu.VMEM((outs, keep), BF16), pltpu.SemaphoreType.DMA],
         name="logit",
@@ -422,7 +449,7 @@
     )(half, z, weight)
 
 
-def back_kernel(mine_ref, other_ref, coef_ref, table_ref, out_ref):
+def back_kernel(mine_ref, other_ref, coef_ref, table_ref, out_ref, wide_ref):
     groups = table_ref.shape[0] // GROUP
     patches = mine_ref.shape[0]
     squashed = jnp.tanh(mine_ref[...] + other_ref[...])
@@ -432,8 +459,14 @@
     )
     wide = jnp.broadcast_to(wide[:, None, :], (patches, groups, groups * GROUP))
     wide = wide.reshape(patches * groups, groups * GROUP)
-    wide = jnp.where(group_masks(patches * groups, groups), wide, 0.0).astype(BF16)
-    out_ref[...] = jnp.dot(wide, table_ref[...], preferred_element_type=F32).astype(BF16)
+    wide_ref[...] = jnp.where(group_masks(patches * groups, groups), wide, 0.0).astype(BF16)
+
+    @pl.loop(0, out_ref.shape[1] // 512)
+    def _(i):
+        lanes = pl.ds(pl.multiple_of(i * 512, 128), 512)
+        out_ref[:, lanes] = jnp.dot(
+            wide_ref[...], table_ref[:, lanes], preferred_element_type=F32
+        ).astype(BF16)
 
 
 def run_back(mine, other, coef, table):
@@ -443,6 +476,7 @@
         out_shape=jax.ShapeDtypeStruct((rows, table.shape[1]), BF16),
         in_specs=[VM] * 4,
         out_specs=VM,
+        scratch_shapes=[pltpu.VMEM((rows, table.shape[0]), BF16)],
         name="back",
         compiler_params=GRANT,
     )(mine, other, coef, table)
@@ -470,18 +504,20 @@
     half = wa_ref.shape[0] * wa_ref.shape[2]
     cu = wa_ref.shape[3]
 
-    @pl.loop(0, wa_ref.shape[1])
-    def _(tap):
-        total = None
-        for part, w_ref in enumerate((wa_ref, wb_ref)):
-            turned = lax.dot_general(
-                w_ref[:, tap].reshape(half, cu),
-                spread_ref[:, part * half : (part + 1) * half],
-                (((0,), (1,)), ((), ())),
-                preferred_element_type=F32,
-            )
-            total = turned if total is None else total + turned
-        out_ref[tap] = total.astype(BF16)
+    @pl.loop(0, wa_ref.shape[1] // 3)
+    def _(three):
+        for within in range(3):
+            tap = 3 * three + within
+            total = None
+            for part, w_ref in enumerate((wa_ref, wb_ref)):
+                turned = lax.dot_general(
+                    w_ref[:, tap].reshape(half, cu),
+                    spread_ref[:, part * half : (part + 1) * half],
+                    (((0,), (1,)), ((), ())),
+                    preferred_element_type=F32,
+                )
+                total = turned if total is None else total + turned
+            out_ref[tap] = total.astype(BF16)
 
 
 def run_order(wa, wb, spread):
@@ -496,15 +532,13 @@
 
 
 def adj_kernel(pre_ref, w_ref, *rest):
-    *grad_refs, gf_ref, l_ref, r_ref, held, acc_ref, grads = rest
+    grads, gf_ref, l_ref, r_ref, held, acc_ref = rest
     frames, cols, rows, ch = gf_ref.shape
     outer = cols + 2
     cu = w_ref.shape[1]
     block = outer * rows
     held[:, frames * block :, :] = jnp.zeros((9, 2 * block, cu), BF16)
     zero = jnp.zeros((1, rows, cu), F32)
-    for i, grad_ref in enumerate(grad_refs):
-        grads[i] = grad_ref[...]
 
     @pl.loop(0, frames)
     def _(t):
@@ -564,16 +598,15 @@
             jax.ShapeDtypeStruct((frames, 2, rows, ch), BF16),
             jax.ShapeDtypeStruct((frames, 2, rows, ch), BF16),
         ],
-        in_specs=[VM] * (2 + len(grads)),
+        in_specs=[VM] * 3,
         out_specs=[VM] * 3,
         scratch_shapes=[
             pltpu.VMEM((9, 6 * (cols + 2) * rows, cu), BF16),
             pltpu.VMEM((frames * (cols + 2) * rows, ch), F32),
-            pltpu.VMEM(pre.shape, BF16),
         ],
         name="adj",
         compiler_params=GRANT,
-    )(pre, weight, *grads)
+    )(pre, weight, grads)
 
 
 def on_device(latent, frame_order, section_weight, section_gain, up_weight, reward_weight, reward_coef):
@@ -652,7 +685,7 @@
     up_shape = (chips, 27, PAD, cu)
 
     def turn(weight):
-        return weight[0].transpose(0, 2, 1).reshape(27 * ch, ch)
+        return run_turn(weight[0])
 
     def start():
         x, left, right = run_first(frame_order, latent.transpose(0, 2, 1, 3))
@@ -728,9 +761,19 @@
     group = [(s, s // halves * halves + (s + 1) % halves) for s in range(segs)]
     other = lax.ppermute(partial, "segment", group)
     shares = run_back(partial, other, coef, table)
-    shares = lax.all_to_all(shares.reshape(tiles, *chunk), TILE, 0, 0, tiled=True)
+    shares = lax.cond(
+        seg >= 0,
+        lambda: lax.all_to_all(shares.reshape(tiles, *chunk), TILE, 0, 0, tiled=True),
+        lambda: unwritten((tiles, *chunk))[0],
+    )
     share = run_sum(shares)
-    grads = [send(share, k, last) for k in range(last)] + [share]
+    grads = lax.cond(
+        seg >= 0,
+        lambda: lax.all_to_all(
+            jnp.broadcast_to(share[None], (segs, *chunk)), "segment", 0, 0, tiled=True
+        ),
+        lambda: unwritten((segs, *chunk))[0],
+    )
 
     results = {}
     for k in range(last, 0, -1):

time: 293 us -> 291 us (level)
  blocking collectives: 35.6 us -> 56.1 us
  Pallas kernels: 13.4 us -> 27.4 us
  waiting for transfers between devices: 192 us -> 179 us
  starting transfers between devices: 33.7 us -> 21.7 us
  local copies, waits for them, and re-layouts: 15.9 us -> 4.43 us
    all_to_all x0 -> x1, blocking collectives: none -> 20.5 us  [on_device(): lax.all_to_all(jnp.broadcast_to(share[None], (segs, *chunk)), 'segment',...]
    pallas_call x0 -> x1, Pallas kernels: none -> 13.6 us  [run_turn(): pl.pallas_call(turn_kernel, out_shape=jax.ShapeDtypeStruct(weight.shape,...]
    ppermute x14 -> x7, starting transfers between devices: 17.5 us -> 5.44 us  [send(): return lax.ppermute(value, AXES, route([(source, target)], 0))]
    transpose x1 -> x0, local copies, waits for them, and re-layouts: 11.5 us -> none  [turn(): return weight[0].transpose(0, 2, 1).reshape(27 * ch, ch)]
    ppermute x2, waiting for transfers between devices: 109 us -> 98.8 us  [half_hop(): lax.ppermute(last_three, AXES, turn_round(*hop_route(source, target, to_r...]
    ppermute x14 -> x7, waiting for transfers between devices: 78.7 us -> 76 us  [send(): return lax.ppermute(value, AXES, route([(source, target)], 0))]
  transfers between devices with their start and end apart: 21 -> 14, of which waited for: 5 -> 5; matrix products, arithmetic and copies ran while one was open for 0% -> 0% of each run, Pallas kernels for 0% -> 0%
where the time goes in v1:
time: 291 us; the launch traced here: 290 us
  waiting for transfers between devices  179 us (62%)
  blocking collectives  56.1 us (19%)
  Pallas kernels  27.4 us (9%)
  starting transfers between devices  21.7 us (7%)
  local copies, waits for them, and re-layouts  4.43 us (2%)
    ppermute x2, waiting for transfers between devices, half_hop(): lax.ppermute(last_three, AXES, turn_round(*hop_route(source, target, to_r...  98.8 us
    ppermute x7, waiting for transfers between devices, send(): return lax.ppermute(value, AXES, route([(source, target)], 0))  76 us
    all_to_all x1, blocking collectives, on_device(): lax.all_to_all(jnp.broadcast_to(share[None], (segs, *chunk)), 'segment',...  20.5 us
    all_to_all x1, blocking collectives, on_device(): lax.all_to_all(shares.reshape(tiles, *chunk), TILE, 0, 0, tiled=True)  17.8 us
    all_to_all x1, blocking collectives, on_device(): lax.all_to_all(jnp.broadcast_to(mine[None], (tiles, *chunk)), TILE, 0, 0,...  17.8 us
    pallas_call x1, Pallas kernels, run_turn(): pl.pallas_call(turn_kernel, out_shape=jax.ShapeDtypeStruct(weight.shape,...  13.6 us
    ppermute x2, starting transfers between devices, beside(): lax.ppermute(value, AXES, route([(s, s) for s in range(segs)], shift))  7.67 us
  transfers between devices with their start and end apart: 14, of which 5 were waited for; matrix products, arithmetic and copies ran while one was open for 0% of the time, Pallas kernels for 0%

profile of v1, /device:TPU:2, one launch (start us, length us, event | category | flops | bytes accessed | tf_op | source)
XLA Modules:
  0.0 289.8 jit_solution(4757941382667123995)
XLA Ops:
  0.0 0.9 copy-done.3
  0.9 9.8 %conditional.39 = (bf16[4,1,8,384]{3,2,1,0:T(8,128)(2,1)}, bf16[4,4,8,384]{3,2,1,0:T(8,128)(2,1)S(1)}, bf16[4,1,8,384]{3,2,1,0:T(8,128)(2,1)}) conditional(s32[]{:T(128)} %convert_element_type.97, () %tuple.372, (bf16[4,8,4,384]{3,2,1,0:T(4,128)(2,1)S(1)}, s32[4]{0:T(128)S(1)}) %tuple.560), branch_computations={%region_4.5_spmd, %region_5.6_spmd} | conditional | bytes 393320 | solution.py:701
  0.9 0.6 first.1
  1.5 1.9 collective-permute-start.33
  3.4 5.8 %collective-permute-start.34 = (bf16[4,1,8,384]{3,2,1,0:T(8,128)(2,1)S(1)}, bf16[4,1,8,384]{3,2,1,0:T(8,128)(2,1)}, u32[]{:S(2)}, u32[]{:S(2)}) collective-permute-start(bf16[4,1,8,384]{3,2,1,0:T(8,128)(2,1)S(1)} %get-tuple-element.473), channel_id=1, source_target_pairs={{1,0},{2,1},{3,2},{4,3},{5,4},{6,5},{7,6},{8,7},{9,8},{10,9},{11,1... | collective-permute-start | bytes 73736 | tf_op jit(solution)/shard_map/cond/branch_1_fun/ppermute | solution.py:644
  9.2 1.5 collective-permute-done.34
  10.7 0.1 pad_add_fusion
  10.8 0.6 copy-done.1
  11.4 9.8 %conditional.40 = (bf16[4,3,8,384]{3,2,1,0:T(8,128)(2,1)}, bf16[4,3,8,384]{3,2,1,0:T(8,128)(2,1)}) conditional(s32[]{:T(128)} %convert_element_type.98, () %tuple.376, (s32[]{:T(128)}, s32[2]{0:T(128)S(1)}, bf16[4,1,8,384]{3,2,1,0:T(8,128)(2,1)}, bf16[4,4,8,384]{3,2,1,0:T(8,128)(2,1)S(1)}, bf16[4,1,8,384]{3,2,1,0:T(8,128)(2,1)}, ...), branch_computations={%region_6.7_spmd, %region_7.10_spmd} | conditional | flops 2 | bytes 590006 | solution.py:722
  11.4 4.7 %conditional = ((bf16[4,3,8,384]{3,2,1,0:T(8,128)(2,1)S(1)}, bf16[4,3,8,384]{3,2,1,0:T(8,128)(2,1)S(1)})) conditional(s32[]{:T(128)} %convert_element_type.21, () %tuple.249, (s32[2]{0:T(128)S(1)}, bf16[4,1,8,384]{3,2,1,0:T(8,128)(2,1)}, bf16[4,4,8,384]{3,2,1,0:T(8,128)(2,1)S(1)}, bf16[4,1,8,384]{3,2,1,0:T(8,128)(2,1)}, bf16[1,384]{1,0:T(2,128)(2,1)S(1)}, ...), branch_computations={%region_8.8_spmd, %region_9.9_spmd} | conditional | bytes 24 | solution.py:712
  11.4 4.7 %fwd_even.4 = (bf16[4,3,8,384]{3,2,1,0:T(8,128)(2,1)S(1)}, bf16[4,3,8,384]{3,2,1,0:T(8,128)(2,1)S(1)}) custom-call(s32[2]{0:T(128)S(1)} %get-tuple-element.474.refs_0_, bf16[4,1,8,384]{3,2,1,0:T(8,128)(2,1)} %get-tuple-element.475.refs_1_, bf16[4,4,8,384]{3,2,1,0:T(8,128)(2,1)S(1)} %get-tuple-element.476.refs_2_, ...), custom_call_target="tpu_custom_call" | custom-call | tf_op jit(solution)/shard_map/cond/branch_1_fun/cond/branch_1_fun/fwd_even/pallas_call | solution.py:144
  16.1 1.9 collective-permute-start
  18.0 1.9 collective-permute-start.1
  19.9 1.3 collective-permute-done.1
  21.2 13.6 %conditional.42 = (bf16[10368,384]{1,0:T(8,128)(2,1)}) conditional(s32[]{:T(128)} %convert_element_type.100, () %tuple.379, bf16[1,27,384,384]{3,2,1,0:T(8,128)(2,1)} %param.89), branch_computations={%region_14.15_spmd, %region_15.16_spmd} | conditional | bytes 8 | solution.py:728
  21.2 13.6 %turn.3 = bf16[27,384,384]{2,1,0:T(8,128)(2,1)} custom-call(bf16[27,384,384]{2,1,0:T(8,128)(2,1)} %bitcast.55), custom_call_target="tpu_custom_call" | custom-call | tf_op jit(solution)/shard_map/cond/branch_1_fun/turn/pallas_call | solution.py:260
  35.0 0.0 copy-start.5
  35.0 0.1 conditional.48
  35.1 1.3 collective-permute-start.38
  36.4 0.7 collective-permute-start.39
  37.1 0.8 collective-permute-start.40
  37.9 0.7 collective-permute-start.41
  38.6 0.7 collective-permute-start.42
  39.2 75.9 %collective-permute-done.38 = bf16[8,1536]{1,0:T(8,128)(2,1)S(1)} collective-permute-done((bf16[8,1536]{1,0:T(8,128)(2,1)S(1)}, bf16[8,1536]{1,0:T(8,128)(2,1)S(1)}, u32[]{:S(2)}, u32[]{:S(2)}) %collective-permute-start.38) | collective-permute-done | bytes 24608 | tf_op jit(solution)/shard_map/ppermute | solution.py:641
  115.2 0.7 collective-permute-start.43
  115.9 0.7 collective-permute-start.44
  116.6 17.8 %conditional.49 = (bf16[256,1536]{1,0:T(8,128)(2,1)S(1)}) conditional(s32[]{:T(128)} %convert_element_type.106, () %tuple.403, bf16[8,1536]{1,0:T(8,128)(2,1)S(1)} %add_add_fusion), branch_computations={%region_38.39_spmd, %region_39.40_spmd} | conditional | bytes 2383880 | solution.py:752
  116.6 0.1 broadcast_in_dim.43
  116.7 17.8 %all_to_all.17 = bf16[32,8,1536]{2,1,0:T(8,128)(2,1)S(1)} all-to-all(bf16[32,8,1536]{2,1,0:T(8,128)(2,1)S(1)} %broadcast_in_dim.43), channel_id=1, replica_groups=mesh['segment'=8,'chip'=16,'core'=2] {'chip','core'}, dimensions={0} | all-to-all | bytes 1572864 | tf_op jit(solution)/shard_map/cond/branch_1_fun/all_to_all | solution.py:754
  134.5 2.1 copy-done
  136.6 2.0 logit.1
  138.6 2.2 collective-permute-start.45
  140.7 1.6 collective-permute-done.45.other_ref
  142.4 1.5 back.1
  143.9 17.8 %conditional.50 = (bf16[32,8,1536]{2,1,0:T(8,128)(2,1)S(1)}) conditional(s32[]{:T(128)} %convert_element_type.106, () %tuple.402, bf16[256,1536]{1,0:T(8,128)(2,1)S(1)} %back.1), branch_computations={%region_40.41_spmd, %region_41.42_spmd} | conditional | bytes 1572872 | solution.py:764
  143.9 17.8 %all_to_all.18 = bf16[32,8,1536]{2,1,0:T(8,128)(2,1)S(1)} all-to-all(bf16[32,8,1536]{2,1,0:T(8,128)(2,1)S(1)} %bitcast.60), channel_id=1, replica_groups=mesh['segment'=8,'chip'=16,'core'=2] {'chip','core'}, dimensions={0} | all-to-all | bytes 1572864 | tf_op jit(solution)/shard_map/cond/branch_1_fun/all_to_all | solution.py:766
  161.7 0.1 sum.1
  161.8 20.5 %conditional.51 = (bf16[8,8,1536]{2,1,0:T(8,128)(2,1)S(1)}) conditional(s32[]{:T(128)} %convert_element_type.106, () %tuple.401, bf16[8,1536]{1,0:T(8,128)(2,1)S(1)} %sum.1), branch_computations={%region_42.43_spmd, %region_43.44_spmd} | conditional | bytes 614408 | solution.py:770
  161.9 20.5 %all_to_all.19 = bf16[8,8,1536]{2,1,0:T(8,128)(2,1)S(1)} all-to-all(bf16[8,8,1536]{2,1,0:T(8,128)(2,1)S(1)} %broadcast_in_dim.44), channel_id=1, replica_groups=mesh['segment'=8,'chip'=16,'core'=2] {'segment'}, dimensions={0} | all-to-all | bytes 393216 | tf_op jit(solution)/shard_map/cond/branch_1_fun/all_to_all | solution.py:772
  182.6 101.5 %conditional.58 = (bf16[4,3,8,384]{3,2,1,0:T(8,128)(2,1)}, bf16[4,3,8,384]{3,2,1,0:T(8,128)(2,1)}, f32[4,4,8,384]{3,2,1,0:T(8,128)}) conditional(s32[]{:T(128)} %convert_element_type.98, () %tuple.375, (s32[]{:T(128)}, s32[2]{0:T(128)S(1)}, bf16[4,3,8,384]{3,2,1,0:T(8,128)(2,1)}, bf16[4,3,8,384]{3,2,1,0:T(8,128)(2,1)}, ...), branch_computations={%region_68.69_spmd, %region_69.72_spmd} | conditional | flops 2 | bytes 590022 | solution.py:806
  182.6 1.3 collective-permute-start.30
  183.9 1.3 collective-permute-start.31
  185.2 98.8 %collective-permute-done.30 = bf16[4,3,8,384]{3,2,1,0:T(8,128)(2,1)} collective-permute-done((bf16[4,3,8,384]{3,2,1,0:T(8,128)(2,1)S(1)}, bf16[4,3,8,384]{3,2,1,0:T(8,128)(2,1)}, u32[]{:S(2)}, u32[]{:S(2)}) %collective-permute-start.30) | collective-permute-done | bytes 73760 | tf_op jit(solution)/shard_map/cond/branch_1_fun/ppermute | solution.py:667
  284.1 5.0 %conditional.59 = (f32[1,4,8,4,384]{4,3,2,1,0:T(4,128)S(1)}) conditional(s32[]{:T(128)} %clamp.3, (s32[2]{0:T(128)S(1)}, bf16[4,4,8,384]{3,2,1,0:T(8,128)(2,1)S(1)}, bf16[4,3,8,384]{3,2,1,0:T(8,128)(2,1)}, bf16[4,3,8,384]{3,2,1,0:T(8,128)(2,1)}, bf16[1,384]{1,0:T(2,128)(2,1)S(1)}, ...), branch_computations={%region_72.73_spmd, %region_73.74_spmd, %region_74.75_spmd, %regio... | conditional | flops 49152 | bytes 1572912 | solution.py:825
  284.1 4.9 %bwd_even.7 = f32[4,4,8,384]{3,2,1,0:T(8,128)S(1)} custom-call(s32[2]{0:T(128)S(1)} %get-tuple-element.731.refs_0_, bf16[4,4,8,384]{3,2,1,0:T(8,128)(2,1)S(1)} %get-tuple-element.732.refs_1_, bf16[4,3,8,384]{3,2,1,0:T(8,128)(2,1)} %get-tuple-element.733.refs_2_, bf16[4,3,8,384]{3,2,1,0:T(8,128)(2,1)} %get-tuple-element.734.refs_3_, ...), custom_call_target="tpu_custom_call" | custom-call | tf_op jit(solution)/shard_map/cond/branch_0_fun/bwd_even/pallas_call | solution.py:227
  289.0 0.1 copy.22
  289.1 0.0 copy-start.2
  289.1 0.7 copy-done.2
  (83 shorter events, 0.5 us)
Async XLA Ops:
  0.0 0.9 copy-start.3
  0.0 0.9 copy-start.4
  1.5 7.7 %collective-permute-start.33 = (bf16[4,1,8,384]{3,2,1,0:T(8,128)(2,1)S(1)}, bf16[4,1,8,384]{3,2,1,0:T(8,128)(2,1)}, u32[]{:S(2)}, u32[]{:S(2)}) collective-permute-start(bf16[4,1,8,384]{3,2,1,0:T(8,128)(2,1)S(1)} %get-tuple-element.471), channel_id=1, source_target_pairs={{0,1},{1,2},{2,3},{3,4},{4,5},{5,6},{6,7},{7,8},{8,9},{9,10},{10,1... | collective-permute-start | bytes 73736 | tf_op jit(solution)/shard_map/cond/branch_1_fun/ppermute | solution.py:644
  3.4 7.3 %collective-permute-start.34 = (bf16[4,1,8,384]{3,2,1,0:T(8,128)(2,1)S(1)}, bf16[4,1,8,384]{3,2,1,0:T(8,128)(2,1)}, u32[]{:S(2)}, u32[]{:S(2)}) collective-permute-start(bf16[4,1,8,384]{3,2,1,0:T(8,128)(2,1)S(1)} %get-tuple-element.473), channel_id=1, source_target_pairs={{1,0},{2,1},{3,2},{4,3},{5,4},{6,5},{7,6},{8,7},{9,8},{10,9},{11,1... | collective-permute-start | bytes 73736 | tf_op jit(solution)/shard_map/cond/branch_1_fun/ppermute | solution.py:644
  10.7 0.7 copy-start.1
  16.1 3.8 %collective-permute-start = (bf16[4,3,8,384]{3,2,1,0:T(8,128)(2,1)S(1)}, bf16[4,3,8,384]{3,2,1,0:T(8,128)(2,1)}, u32[]{:S(2)}, u32[]{:S(2)}) collective-permute-start(bf16[4,3,8,384]{3,2,1,0:T(8,128)(2,1)S(1)} %get-tuple-element.487), channel_id=1, source_target_pairs={{0,32},{1,33},{2,34},{3,35},{4,36},{5,37},{6,38},{7,39},{8,40},{9,... | collective-permute-start | bytes 221192 | tf_op jit(solution)/shard_map/cond/branch_1_fun/ppermute | solution.py:667
  18.0 3.3 %collective-permute-start.1 = (bf16[4,3,8,384]{3,2,1,0:T(8,128)(2,1)S(1)}, bf16[4,3,8,384]{3,2,1,0:T(8,128)(2,1)}, u32[]{:S(2)}, u32[]{:S(2)}) collective-permute-start(bf16[4,3,8,384]{3,2,1,0:T(8,128)(2,1)S(1)} %get-tuple-element.488), channel_id=1, source_target_pairs={{0,63},{1,32},{2,33},{3,34},{4,35},{5,36},{6,37},{7,38},{8,39},{9,... | collective-permute-start | bytes 221192 | tf_op jit(solution)/shard_map/cond/branch_1_fun/ppermute | solution.py:668
  35.0 81.6 %copy-start.5 = (f32[40]{0:T(128)S(1)}, f32[40]{0:T(128)}, u32[]{:S(2)}) copy-start(f32[40]{0:T(128)} %param.93) | copy-start | bytes 484
  35.1 80.1 %collective-permute-start.38 = (bf16[8,1536]{1,0:T(8,128)(2,1)S(1)}, bf16[8,1536]{1,0:T(8,128)(2,1)S(1)}, u32[]{:S(2)}, u32[]{:S(2)}) collective-permute-start(bf16[8,1536]{1,0:T(8,128)(2,1)S(1)} %get-tuple-element.844), channel_id=1, source_target_pairs={{224,0},{225,1},{226,2},{227,3},{228,4},{229,5},{230,6},{231,7},{2... | collective-permute-start | bytes 73736 | tf_op jit(solution)/shard_map/ppermute | solution.py:641
  36.4 79.5 %collective-permute-start.39 = (bf16[8,1536]{1,0:T(8,128)(2,1)S(1)}, bf16[8,1536]{1,0:T(8,128)(2,1)S(1)}, u32[]{:S(2)}, u32[]{:S(2)}) collective-permute-start(bf16[8,1536]{1,0:T(8,128)(2,1)S(1)} %get-tuple-element.845), channel_id=1, source_target_pairs={{224,32},{225,33},{226,34},{227,35},{228,36},{229,37},{230,38},{23... | collective-permute-start | bytes 73736 | tf_op jit(solution)/shard_map/ppermute | solution.py:641
  37.1 79.5 %collective-permute-start.40 = (bf16[8,1536]{1,0:T(8,128)(2,1)S(1)}, bf16[8,1536]{1,0:T(8,128)(2,1)S(1)}, u32[]{:S(2)}, u32[]{:S(2)}) collective-permute-start(bf16[8,1536]{1,0:T(8,128)(2,1)S(1)} %get-tuple-element.846), channel_id=1, source_target_pairs={{224,64},{225,65},{226,66},{227,67},{228,68},{229,69},{230,70},{23... | collective-permute-start | bytes 73736 | tf_op jit(solution)/shard_map/ppermute | solution.py:641
  37.9 78.7 %collective-permute-start.41 = (bf16[8,1536]{1,0:T(8,128)(2,1)S(1)}, bf16[8,1536]{1,0:T(8,128)(2,1)S(1)}, u32[]{:S(2)}, u32[]{:S(2)}) collective-permute-start(bf16[8,1536]{1,0:T(8,128)(2,1)S(1)} %get-tuple-element.847), channel_id=1, source_target_pairs={{224,96},{225,97},{226,98},{227,99},{228,100},{229,101},{230,102},... | collective-permute-start | bytes 73736 | tf_op jit(solution)/shard_map/ppermute | solution.py:641
  38.6 78.0 %collective-permute-start.42 = (bf16[8,1536]{1,0:T(8,128)(2,1)S(1)}, bf16[8,1536]{1,0:T(8,128)(2,1)S(1)}, u32[]{:S(2)}, u32[]{:S(2)}) collective-permute-start(bf16[8,1536]{1,0:T(8,128)(2,1)S(1)} %get-tuple-element.848), channel_id=1, source_target_pairs={{224,128},{225,129},{226,130},{227,131},{228,132},{229,133},{230,1... | collective-permute-start | bytes 73736 | tf_op jit(solution)/shard_map/ppermute | solution.py:641
  115.2 1.4 collective-permute-start.43
  115.9 0.7 collective-permute-start.44
  134.5 2.1 copy-start
  138.6 3.8 %collective-permute-start.45 = (f32[16,48]{1,0:T(8,128)S(1)}, f32[16,48]{1,0:T(8,128)S(1)}, u32[]{:S(2)}, u32[]{:S(2)}) collective-permute-start(f32[16,48]{1,0:T(8,128)S(1)} %get-tuple-element.852.mine_ref), channel_id=1, source_target_pairs={{0,32},{32,0},{64,96},{96,64},{128,160},{160,128},{192,224},{224,1... | collective-permute-start | bytes 9224 | tf_op jit(solution)/shard_map/ppermute | solution.py:762
  182.6 101.4 %collective-permute-start.30 = (bf16[4,3,8,384]{3,2,1,0:T(8,128)(2,1)S(1)}, bf16[4,3,8,384]{3,2,1,0:T(8,128)(2,1)}, u32[]{:S(2)}, u32[]{:S(2)}) collective-permute-start(bf16[4,3,8,384]{3,2,1,0:T(8,128)(2,1)S(1)} %get-tuple-element.728), channel_id=1, source_target_pairs={{32,1},{33,2},{34,3},{35,4},{36,5},{37,6},{38,7},{39,8},{40,9},{41... | collective-permute-start | bytes 221192 | tf_op jit(solution)/shard_map/cond/branch_1_fun/ppermute | solution.py:667
  183.9 100.1 %collective-permute-start.31 = (bf16[4,3,8,384]{3,2,1,0:T(8,128)(2,1)S(1)}, bf16[4,3,8,384]{3,2,1,0:T(8,128)(2,1)}, u32[]{:S(2)}, u32[]{:S(2)}) collective-permute-start(bf16[4,3,8,384]{3,2,1,0:T(8,128)(2,1)S(1)} %get-tuple-element.729), channel_id=1, source_target_pairs={{32,0},{33,1},{34,2},{35,3},{36,4},{37,5},{38,6},{39,7},{40,8},{41... | collective-permute-start | bytes 221192 | tf_op jit(solution)/shard_map/cond/branch_1_fun/ppermute | solution.py:668
  289.1 0.7 copy-start.2

commit v2 on v1

--- a/solution.py
+++ b/solution.py
@@ -41,6 +41,29 @@
     for step in range(PIECES):
         a = 2 - step // per if backward else step // per
         weight_copy(w_hbm, w_buf, sem, a * per + step % per).start()
+
+
+def convolve_turned(taps, w_hbm, w_buf, sem, acc_ref):
+    count = acc_ref.shape[0]
+    block = count // 4
+    per = PIECES // 3
+    ch = w_hbm.shape[1]
+    acc_ref[...] = jnp.zeros_like(acc_ref)
+
+    @pl.loop(0, 3)
+    def _(step):
+        a = 2 - step
+        for part in range(per):
+            weight_copy(w_hbm, w_buf, sem, a * per + part).wait()
+        total = acc_ref[...]
+        for tap in range(9):
+            total = total + lax.dot_general(
+                taps[pl.ds(pl.multiple_of(step * block, 16), count), tap * ch : (tap + 1) * ch],
+                w_buf[pl.ds(pl.multiple_of((9 * a + tap) * ch, 128), ch), :],
+                (((1,), (1,)), ((), ())),
+                preferred_element_type=F32,
+            )
+        acc_ref[...] = total
 
 
 def convolve(taps, w_hbm, w_buf, sem, acc_ref, backward):
@@ -200,14 +223,16 @@
         before, after = row_shifts(g)
         for b, v in enumerate((after, g, before)):
             put_taps(taps, t, v, b, cols, ch, high if form == "odd" else None, True)
-    @pl.loop(0, frames)
-    def _(t):
+    for t in range(frames):
         x = inputs(t)
         inv = lax.rsqrt(jnp.mean(x * x, axis=-1, keepdims=True) + EPS)
         u = x * inv * gain
         sig = jax.nn.sigmoid(u)
         fac_ref[t] = sig * (1.0 + u * (1.0 - sig)) * gain * inv
-    convolve(taps, w_hbm, w_buf, sem, acc, True)
+    if form == "first":
+        convolve_turned(taps, w_hbm, w_buf, sem, acc)
+    else:
+        convolve(taps, w_hbm, w_buf, sem, acc, True)
     for t in range(frames):
         x = inputs(t)
         inv2 = 1.0 / (jnp.mean(x * x, axis=-1, keepdims=True) + EPS)
@@ -241,33 +266,6 @@
     )(tile_info, *xs, *gs, gain, weight_back)
 
 
-def turn_kernel(in_ref, out_ref):
-    size = in_ref.shape[1]
-    row = lax.broadcasted_iota(jnp.int32, (size, size), 0)
-    lane = lax.broadcasted_iota(jnp.int32, (size, size), 1)
-    same = (row == lane).astype(F32).astype(BF16)
-
-    @pl.loop(0, in_ref.shape[0])
-    def _(i):
-        out_ref[i] = lax.dot_general(
-            same, in_ref[i], (((1,), (1,)), ((), ())), preferred_element_type=F32
-        ).astype(BF16)
-
-
-def run_turn(weight):
-    taps, ch, _ = weight.shape
-    spec = pl.BlockSpec((3, ch, ch), lambda i: (i, 0, 0))
-    return pl.pallas_call(
-        turn_kernel,
-        out_shape=jax.ShapeDtypeStruct(weight.shape, BF16),
-        grid=(taps // 3,),
-        in_specs=[spec],
-        out_specs=spec,
-        name="turn",
-        compiler_params=GRANT,
-    )(weight).reshape(taps * ch, ch)
-
-
 def first_kernel(order_ref, latent_ref, x_ref, l_ref, r_ref):
     for t in range(x_ref.shape[0]):
         x = latent_ref[order_ref[t]]
@@ -313,17 +311,19 @@
             x_ref[t].reshape(block, ch), spread_ref[...], preferred_element_type=F32
         ).astype(BF16)
 
-    @pl.loop(0, 9)
-    def _(tap):
-        total = jnp.zeros((frames * block, cu), F32)
-        for a in range(3):
-            for part, w_ref in enumerate((wa_ref, wb_ref)):
-                total = total + jnp.dot(
-                    held[a * block : (a + frames) * block, part * half : (part + 1) * half],
-                    w_ref[:, 9 * a + tap].reshape(half, cu),
-                    preferred_element_type=F32,
-                )
-        cells[tap] = total
+    @pl.loop(0, 3)
+    def _(three):
+        for within in range(3):
+            tap = 3 * three + within
+            total = jnp.zeros((frames * block, cu), F32)
+            for a in range(3):
+                for part, w_ref in enumerate((wa_ref, wb_ref)):
+                    total = total + jnp.dot(
+                        held[a * block : (a + frames) * block, part * half : (part + 1) * half],
+                        w_ref[:, 9 * a + tap].reshape(half, cu),
+                        preferred_element_type=F32,
+                    )
+            cells[tap] = total
 
     shape = (frames, outer, rows, cu)
     by_phase = [[], []]
@@ -685,7 +685,7 @@
     up_shape = (chips, 27, PAD, cu)
 
     def turn(weight):
-        return run_turn(weight[0])
+        return weight[0].transpose(0, 2, 1).reshape(27 * ch, ch)
 
     def start():
         x, left, right = run_first(frame_order, latent.transpose(0, 2, 1, 3))
@@ -697,7 +697,7 @@
         gather_up,
         lambda: unwritten(up_shape, up_shape, (ch, tiles * PAD), (27, cu, ch)),
     )
-    turned = lax.cond(seg > 1, lambda: turn(section_weight), lambda: unwritten((27 * ch, ch))[0])
+    turned = lax.cond((seg > 1) & (seg < last), lambda: turn(section_weight), lambda: unwritten((27 * ch, ch))[0])
     state = lax.cond(seg == 0, start, lambda: unwritten(side, block, side))
     gathered, turned, state = barrier((gathered, turned, state))
 
@@ -785,7 +785,7 @@
                     from_r, from_l = beside(lp, -1), beside(rp, 1)
                     gs = (deep, lp, rp, from_l, from_r)
                     made = run_bwd(
-                        "first", (cols, 1, 1), tile_info, taken[k][1:2], gs, section_gain, turned
+                        "first", (cols, 1, 1), tile_info, taken[k][1:2], gs, section_gain, weight_fwd
                     )
                 else:
                     form = "odd" if k % 2 else "even"

time: 291 us -> 289 us (level)
  Pallas kernels: 27.4 us -> 13.8 us
  local copies, waits for them, and re-layouts: 4.43 us -> 16.2 us
    pallas_call x1 -> x0, Pallas kernels: 13.6 us -> none  [run_turn(): pl.pallas_call(turn_kernel, out_shape=jax.ShapeDtypeStruct(weight.shape,...]
    transpose x0 -> x1, local copies, waits for them, and re-layouts: none -> 11.5 us  [turn(): return weight[0].transpose(0, 2, 1).reshape(27 * ch, ch)]
where the time goes in v2:
time: 289 us; the launch traced here: 288 us
  waiting for transfers between devices  179 us (62%)
  blocking collectives  56.2 us (19%)
  starting transfers between devices  21.5 us (7%)
  local copies, waits for them, and re-layouts  16.2 us (6%)
  Pallas kernels  13.8 us (5%)
    ppermute x2, waiting for transfers between devices, half_hop(): lax.ppermute(last_three, AXES, turn_round(*hop_route(source, target, to_r...  99.5 us
    ppermute x7, waiting for transfers between devices, send(): return lax.ppermute(value, AXES, route([(source, target)], 0))  74.7 us
    all_to_all x1, blocking collectives, on_device(): lax.all_to_all(jnp.broadcast_to(share[None], (segs, *chunk)), 'segment',...  20.3 us
    all_to_all x1, blocking collectives, on_device(): lax.all_to_all(jnp.broadcast_to(mine[None], (tiles, *chunk)), TILE, 0, 0,...  18.1 us
    all_to_all x1, blocking collectives, on_device(): lax.all_to_all(shares.reshape(tiles, *chunk), TILE, 0, 0, tiled=True)  17.8 us
    transpose x1, local copies, waits for them, and re-layouts, turn(): return weight[0].transpose(0, 2, 1).reshape(27 * ch, ch)  11.5 us
    ppermute x2, starting transfers between devices, beside(): lax.ppermute(value, AXES, route([(s, s) for s in range(segs)], shift))  7.67 us
  transfers between devices with their start and end apart: 14, of which 5 were waited for; matrix products, arithmetic and copies ran while one was open for 0% of the time, Pallas kernels for 0%

profile of v2, /device:TPU:2, one launch (start us, length us, event | category | flops | bytes accessed | tf_op | source)
XLA Modules:
  0.0 287.8 jit_solution(621497260795864918)
XLA Ops:
  0.0 0.9 copy-done.2
  0.9 0.9 copy-done.4
  1.8 9.8 %conditional.39 = (bf16[4,1,8,384]{3,2,1,0:T(8,128)(2,1)}, bf16[4,4,8,384]{3,2,1,0:T(8,128)(2,1)S(1)}, bf16[4,1,8,384]{3,2,1,0:T(8,128)(2,1)}) conditional(s32[]{:T(128)} %convert_element_type.97, () %tuple.372, (bf16[4,8,4,384]{3,2,1,0:T(4,128)(2,1)S(1)}, s32[4]{0:T(128)S(1)}) %tuple.562), branch_computations={%region_4.5_spmd, %region_5.6_spmd} | conditional | bytes 393320 | solution.py:701
  1.9 0.6 first.1
  2.4 1.9 collective-permute-start.33
  4.4 5.8 %collective-permute-start.34 = (bf16[4,1,8,384]{3,2,1,0:T(8,128)(2,1)S(1)}, bf16[4,1,8,384]{3,2,1,0:T(8,128)(2,1)}, u32[]{:S(2)}, u32[]{:S(2)}) collective-permute-start(bf16[4,1,8,384]{3,2,1,0:T(8,128)(2,1)S(1)} %get-tuple-element.473), channel_id=1, source_target_pairs={{1,0},{2,1},{3,2},{4,3},{5,4},{6,5},{7,6},{8,7},{9,8},{10,9},{11,1... | collective-permute-start | bytes 73736 | tf_op jit(solution)/shard_map/cond/branch_1_fun/ppermute | solution.py:644
  10.1 1.5 collective-permute-done.34
  11.6 0.1 pad_add_fusion
  11.7 9.9 %conditional.40 = (bf16[4,3,8,384]{3,2,1,0:T(8,128)(2,1)}, bf16[4,3,8,384]{3,2,1,0:T(8,128)(2,1)}) conditional(s32[]{:T(128)} %convert_element_type.98, () %tuple.376, (s32[]{:T(128)}, s32[2]{0:T(128)S(1)}, bf16[4,1,8,384]{3,2,1,0:T(8,128)(2,1)}, bf16[4,4,8,384]{3,2,1,0:T(8,128)(2,1)S(1)}, bf16[4,1,8,384]{3,2,1,0:T(8,128)(2,1)}, ...), branch_computations={%region_6.7_spmd, %region_7.10_spmd} | conditional | flops 2 | bytes 590006 | solution.py:722
  11.7 4.7 %conditional = ((bf16[4,3,8,384]{3,2,1,0:T(8,128)(2,1)S(1)}, bf16[4,3,8,384]{3,2,1,0:T(8,128)(2,1)S(1)})) conditional(s32[]{:T(128)} %convert_element_type.21, () %tuple.249, (s32[2]{0:T(128)S(1)}, bf16[4,1,8,384]{3,2,1,0:T(8,128)(2,1)}, bf16[4,4,8,384]{3,2,1,0:T(8,128)(2,1)S(1)}, bf16[4,1,8,384]{3,2,1,0:T(8,128)(2,1)}, bf16[1,384]{1,0:T(2,128)(2,1)S(1)}, ...), branch_computations={%region_8.8_spmd, %region_9.9_spmd} | conditional | bytes 24 | solution.py:712
  11.7 4.7 %fwd_even.4 = (bf16[4,3,8,384]{3,2,1,0:T(8,128)(2,1)S(1)}, bf16[4,3,8,384]{3,2,1,0:T(8,128)(2,1)S(1)}) custom-call(s32[2]{0:T(128)S(1)} %get-tuple-element.474.refs_0_, bf16[4,1,8,384]{3,2,1,0:T(8,128)(2,1)} %get-tuple-element.475.refs_1_, bf16[4,4,8,384]{3,2,1,0:T(8,128)(2,1)S(1)} %get-tuple-element.476.refs_2_, ...), custom_call_target="tpu_custom_call" | custom-call | tf_op jit(solution)/shard_map/cond/branch_1_fun/cond/branch_1_fun/fwd_even/pallas_call | solution.py:167
  16.4 1.9 collective-permute-start
  18.3 1.9 collective-permute-start.1
  20.2 1.3 collective-permute-done.1
  21.6 11.5 %conditional.42 = (bf16[10368,384]{1,0:T(8,128)(2,1)}) conditional(s32[]{:T(128)} %convert_element_type.100, () %tuple.379, bf16[1,27,384,384]{3,2,1,0:T(8,128)(2,1)} %param.89), branch_computations={%region_14.15_spmd, %region_15.16_spmd} | conditional | bytes 15925256 | solution.py:728
  21.6 11.5 %copy.20 = bf16[27,384,384]{2,1,0:T(8,128)(2,1)} copy(bf16[27,384,384]{1,2,0:T(8,128)(2,1)} %bitcast.60) | data formatting | bytes 15925248 | tf_op jit(solution)/shard_map/cond/branch_1_fun/transpose | solution.py:688
  33.2 0.0 copy-start.6
  33.2 0.3 conditional.48
  33.5 1.3 collective-permute-start.38
  34.8 0.7 collective-permute-start.39
  35.4 0.7 collective-permute-start.40
  36.1 0.7 collective-permute-start.41
  36.8 0.7 collective-permute-start.42
  37.4 74.7 %collective-permute-done.38 = bf16[8,1536]{1,0:T(8,128)(2,1)S(1)} collective-permute-done((bf16[8,1536]{1,0:T(8,128)(2,1)S(1)}, bf16[8,1536]{1,0:T(8,128)(2,1)S(1)}, u32[]{:S(2)}, u32[]{:S(2)}) %collective-permute-start.38) | collective-permute-done | bytes 24608 | tf_op jit(solution)/shard_map/ppermute | solution.py:641
  112.2 0.7 collective-permute-start.43
  112.8 0.7 collective-permute-start.44
  113.6 18.2 %conditional.49 = (bf16[256,1536]{1,0:T(8,128)(2,1)S(1)}) conditional(s32[]{:T(128)} %convert_element_type.106, () %tuple.403, bf16[8,1536]{1,0:T(8,128)(2,1)S(1)} %add_add_fusion), branch_computations={%region_38.39_spmd, %region_39.40_spmd} | conditional | bytes 2383880 | solution.py:752
  113.6 0.1 broadcast_in_dim.43
  113.7 18.1 %all_to_all.17 = bf16[32,8,1536]{2,1,0:T(8,128)(2,1)S(1)} all-to-all(bf16[32,8,1536]{2,1,0:T(8,128)(2,1)S(1)} %broadcast_in_dim.43), channel_id=1, replica_groups=mesh['segment'=8,'chip'=16,'core'=2] {'chip','core'}, dimensions={0} | all-to-all | bytes 1572864 | tf_op jit(solution)/shard_map/cond/branch_1_fun/all_to_all | solution.py:754
  131.8 2.1 copy-done
  133.9 2.0 logit.1
  135.9 2.2 collective-permute-start.45
  138.1 1.6 collective-permute-done.45.other_ref
  139.7 1.5 back.1
  141.2 17.8 %conditional.50 = (bf16[32,8,1536]{2,1,0:T(8,128)(2,1)S(1)}) conditional(s32[]{:T(128)} %convert_element_type.106, () %tuple.402, bf16[256,1536]{1,0:T(8,128)(2,1)S(1)} %back.1), branch_computations={%region_40.41_spmd, %region_41.42_spmd} | conditional | bytes 1572872 | solution.py:764
  141.3 17.8 %all_to_all.18 = bf16[32,8,1536]{2,1,0:T(8,128)(2,1)S(1)} all-to-all(bf16[32,8,1536]{2,1,0:T(8,128)(2,1)S(1)} %bitcast.65), channel_id=1, replica_groups=mesh['segment'=8,'chip'=16,'core'=2] {'chip','core'}, dimensions={0} | all-to-all | bytes 1572864 | tf_op jit(solution)/shard_map/cond/branch_1_fun/all_to_all | solution.py:766
  159.1 0.1 sum.1
  159.2 20.3 %conditional.51 = (bf16[8,8,1536]{2,1,0:T(8,128)(2,1)S(1)}) conditional(s32[]{:T(128)} %convert_element_type.106, () %tuple.401, bf16[8,1536]{1,0:T(8,128)(2,1)S(1)} %sum.1), branch_computations={%region_42.43_spmd, %region_43.44_spmd} | conditional | bytes 614408 | solution.py:770
  159.2 20.3 %all_to_all.19 = bf16[8,8,1536]{2,1,0:T(8,128)(2,1)S(1)} all-to-all(bf16[8,8,1536]{2,1,0:T(8,128)(2,1)S(1)} %broadcast_in_dim.44), channel_id=1, replica_groups=mesh['segment'=8,'chip'=16,'core'=2] {'segment'}, dimensions={0} | all-to-all | bytes 393216 | tf_op jit(solution)/shard_map/cond/branch_1_fun/all_to_all | solution.py:772
  179.6 0.3 conditional.56
  180.0 102.2 %conditional.58 = (bf16[4,3,8,384]{3,2,1,0:T(8,128)(2,1)}, bf16[4,3,8,384]{3,2,1,0:T(8,128)(2,1)}, f32[4,4,8,384]{3,2,1,0:T(8,128)}) conditional(s32[]{:T(128)} %convert_element_type.98, () %tuple.375, (s32[]{:T(128)}, s32[2]{0:T(128)S(1)}, bf16[4,3,8,384]{3,2,1,0:T(8,128)(2,1)}, bf16[4,3,8,384]{3,2,1,0:T(8,128)(2,1)}, ...), branch_computations={%region_68.69_spmd, %region_69.72_spmd} | conditional | flops 2 | bytes 590022 | solution.py:806
  180.0 1.3 collective-permute-start.30
  181.3 1.3 collective-permute-start.31
  182.6 99.5 %collective-permute-done.30 = bf16[4,3,8,384]{3,2,1,0:T(8,128)(2,1)} collective-permute-done((bf16[4,3,8,384]{3,2,1,0:T(8,128)(2,1)S(1)}, bf16[4,3,8,384]{3,2,1,0:T(8,128)(2,1)}, u32[]{:S(2)}, u32[]{:S(2)}) %collective-permute-start.30) | collective-permute-done | bytes 73760 | tf_op jit(solution)/shard_map/cond/branch_1_fun/ppermute | solution.py:667
  282.1 5.0 %conditional.59 = (f32[1,4,8,4,384]{4,3,2,1,0:T(4,128)S(1)}) conditional(s32[]{:T(128)} %clamp.3, (s32[2]{0:T(128)S(1)}, bf16[4,4,8,384]{3,2,1,0:T(8,128)(2,1)S(1)}, bf16[4,3,8,384]{3,2,1,0:T(8,128)(2,1)}, bf16[4,3,8,384]{3,2,1,0:T(8,128)(2,1)}, bf16[1,384]{1,0:T(2,128)(2,1)S(1)}, ...), branch_computations={%region_72.73_spmd, %region_73.74_spmd, %region_74.75_spmd, %regio... | conditional | flops 49152 | bytes 1572912 | solution.py:825
  282.1 4.9 %bwd_even.7 = f32[4,4,8,384]{3,2,1,0:T(8,128)S(1)} custom-call(s32[2]{0:T(128)S(1)} %get-tuple-element.731.refs_0_, bf16[4,4,8,384]{3,2,1,0:T(8,128)(2,1)S(1)} %get-tuple-element.732.refs_1_, bf16[4,3,8,384]{3,2,1,0:T(8,128)(2,1)} %get-tuple-element.733.refs_2_, bf16[4,3,8,384]{3,2,1,0:T(8,128)(2,1)} %get-tuple-element.734.refs_3_, ...), custom_call_target="tpu_custom_call" | custom-call | tf_op jit(solution)/shard_map/cond/branch_0_fun/bwd_even/pallas_call | solution.py:252
  287.0 0.1 copy.24
  287.1 0.7 copy-done.3
  (85 shorter events, 0.5 us)
Async XLA Ops:
  0.0 0.9 copy-start.2
  0.9 0.9 copy-start.4
  0.9 0.9 copy-start.5
  0.9 10.8 %copy-start.1 = (bf16[1,384]{1,0:T(2,128)(2,1)S(1)}, bf16[1,384]{1,0:T(2,128)(2,1)}, u32[]{:S(2)}) copy-start(bf16[1,384]{1,0:T(2,128)(2,1)} %param.90) | copy-start | bytes 2308
  2.4 7.7 %collective-permute-start.33 = (bf16[4,1,8,384]{3,2,1,0:T(8,128)(2,1)S(1)}, bf16[4,1,8,384]{3,2,1,0:T(8,128)(2,1)}, u32[]{:S(2)}, u32[]{:S(2)}) collective-permute-start(bf16[4,1,8,384]{3,2,1,0:T(8,128)(2,1)S(1)} %get-tuple-element.471), channel_id=1, source_target_pairs={{0,1},{1,2},{2,3},{3,4},{4,5},{5,6},{6,7},{7,8},{8,9},{9,10},{10,1... | collective-permute-start | bytes 73736 | tf_op jit(solution)/shard_map/cond/branch_1_fun/ppermute | solution.py:644
  4.4 7.3 %collective-permute-start.34 = (bf16[4,1,8,384]{3,2,1,0:T(8,128)(2,1)S(1)}, bf16[4,1,8,384]{3,2,1,0:T(8,128)(2,1)}, u32[]{:S(2)}, u32[]{:S(2)}) collective-permute-start(bf16[4,1,8,384]{3,2,1,0:T(8,128)(2,1)S(1)} %get-tuple-element.473), channel_id=1, source_target_pairs={{1,0},{2,1},{3,2},{4,3},{5,4},{6,5},{7,6},{8,7},{9,8},{10,9},{11,1... | collective-permute-start | bytes 73736 | tf_op jit(solution)/shard_map/cond/branch_1_fun/ppermute | solution.py:644
  16.4 3.8 %collective-permute-start = (bf16[4,3,8,384]{3,2,1,0:T(8,128)(2,1)S(1)}, bf16[4,3,8,384]{3,2,1,0:T(8,128)(2,1)}, u32[]{:S(2)}, u32[]{:S(2)}) collective-permute-start(bf16[4,3,8,384]{3,2,1,0:T(8,128)(2,1)S(1)} %get-tuple-element.487), channel_id=1, source_target_pairs={{0,32},{1,33},{2,34},{3,35},{4,36},{5,37},{6,38},{7,39},{8,40},{9,... | collective-permute-start | bytes 221192 | tf_op jit(solution)/shard_map/cond/branch_1_fun/ppermute | solution.py:667
  18.3 3.3 %collective-permute-start.1 = (bf16[4,3,8,384]{3,2,1,0:T(8,128)(2,1)S(1)}, bf16[4,3,8,384]{3,2,1,0:T(8,128)(2,1)}, u32[]{:S(2)}, u32[]{:S(2)}) collective-permute-start(bf16[4,3,8,384]{3,2,1,0:T(8,128)(2,1)S(1)} %get-tuple-element.488), channel_id=1, source_target_pairs={{0,63},{1,32},{2,33},{3,34},{4,35},{5,36},{6,37},{7,38},{8,39},{9,... | collective-permute-start | bytes 221192 | tf_op jit(solution)/shard_map/cond/branch_1_fun/ppermute | solution.py:668
  33.2 80.4 %copy-start.6 = (f32[40]{0:T(128)S(1)}, f32[40]{0:T(128)}, u32[]{:S(2)}) copy-start(f32[40]{0:T(128)} %param.93) | copy-start | bytes 484
  33.5 78.7 %collective-permute-start.38 = (bf16[8,1536]{1,0:T(8,128)(2,1)S(1)}, bf16[8,1536]{1,0:T(8,128)(2,1)S(1)}, u32[]{:S(2)}, u32[]{:S(2)}) collective-permute-start(bf16[8,1536]{1,0:T(8,128)(2,1)S(1)} %get-tuple-element.844), channel_id=1, source_target_pairs={{224,0},{225,1},{226,2},{227,3},{228,4},{229,5},{230,6},{231,7},{2... | collective-permute-start | bytes 73736 | tf_op jit(solution)/shard_map/ppermute | solution.py:641
  34.8 78.1 %collective-permute-start.39 = (bf16[8,1536]{1,0:T(8,128)(2,1)S(1)}, bf16[8,1536]{1,0:T(8,128)(2,1)S(1)}, u32[]{:S(2)}, u32[]{:S(2)}) collective-permute-start(bf16[8,1536]{1,0:T(8,128)(2,1)S(1)} %get-tuple-element.845), channel_id=1, source_target_pairs={{224,32},{225,33},{226,34},{227,35},{228,36},{229,37},{230,38},{23... | collective-permute-start | bytes 73736 | tf_op jit(solution)/shard_map/ppermute | solution.py:641
  35.4 78.1 %collective-permute-start.40 = (bf16[8,1536]{1,0:T(8,128)(2,1)S(1)}, bf16[8,1536]{1,0:T(8,128)(2,1)S(1)}, u32[]{:S(2)}, u32[]{:S(2)}) collective-permute-start(bf16[8,1536]{1,0:T(8,128)(2,1)S(1)} %get-tuple-element.846), channel_id=1, source_target_pairs={{224,64},{225,65},{226,66},{227,67},{228,68},{229,69},{230,70},{23... | collective-permute-start | bytes 73736 | tf_op jit(solution)/shard_map/ppermute | solution.py:641
  36.1 77.5 %collective-permute-start.41 = (bf16[8,1536]{1,0:T(8,128)(2,1)S(1)}, bf16[8,1536]{1,0:T(8,128)(2,1)S(1)}, u32[]{:S(2)}, u32[]{:S(2)}) collective-permute-start(bf16[8,1536]{1,0:T(8,128)(2,1)S(1)} %get-tuple-element.847), channel_id=1, source_target_pairs={{224,96},{225,97},{226,98},{227,99},{228,100},{229,101},{230,102},... | collective-permute-start | bytes 73736 | tf_op jit(solution)/shard_map/ppermute | solution.py:641
  36.8 76.8 %collective-permute-start.42 = (bf16[8,1536]{1,0:T(8,128)(2,1)S(1)}, bf16[8,1536]{1,0:T(8,128)(2,1)S(1)}, u32[]{:S(2)}, u32[]{:S(2)}) collective-permute-start(bf16[8,1536]{1,0:T(8,128)(2,1)S(1)} %get-tuple-element.848), channel_id=1, source_target_pairs={{224,128},{225,129},{226,130},{227,131},{228,132},{229,133},{230,1... | collective-permute-start | bytes 73736 | tf_op jit(solution)/shard_map/ppermute | solution.py:641
  112.2 1.4 collective-permute-start.43
  112.8 0.7 collective-permute-start.44
  131.8 2.1 copy-start
  135.9 3.8 %collective-permute-start.45 = (f32[16,48]{1,0:T(8,128)S(1)}, f32[16,48]{1,0:T(8,128)S(1)}, u32[]{:S(2)}, u32[]{:S(2)}) collective-permute-start(f32[16,48]{1,0:T(8,128)S(1)} %get-tuple-element.852.mine_ref), channel_id=1, source_target_pairs={{0,32},{32,0},{64,96},{96,64},{128,160},{160,128},{192,224},{224,1... | collective-permute-start | bytes 9224 | tf_op jit(solution)/shard_map/ppermute | solution.py:762
  180.0 102.1 %collective-permute-start.30 = (bf16[4,3,8,384]{3,2,1,0:T(8,128)(2,1)S(1)}, bf16[4,3,8,384]{3,2,1,0:T(8,128)(2,1)}, u32[]{:S(2)}, u32[]{:S(2)}) collective-permute-start(bf16[4,3,8,384]{3,2,1,0:T(8,128)(2,1)S(1)} %get-tuple-element.728), channel_id=1, source_target_pairs={{32,1},{33,2},{34,3},{35,4},{36,5},{37,6},{38,7},{39,8},{40,9},{41... | collective-permute-start | bytes 221192 | tf_op jit(solution)/shard_map/cond/branch_1_fun/ppermute | solution.py:667
  181.3 100.8 %collective-permute-start.31 = (bf16[4,3,8,384]{3,2,1,0:T(8,128)(2,1)S(1)}, bf16[4,3,8,384]{3,2,1,0:T(8,128)(2,1)}, u32[]{:S(2)}, u32[]{:S(2)}) collective-permute-start(bf16[4,3,8,384]{3,2,1,0:T(8,128)(2,1)S(1)} %get-tuple-element.729), channel_id=1, source_target_pairs={{32,0},{33,1},{34,2},{35,3},{36,4},{37,5},{38,6},{39,7},{40,8},{41... | collective-permute-start | bytes 221192 | tf_op jit(solution)/shard_map/cond/branch_1_fun/ppermute | solution.py:668
  287.1 0.7 copy-start.3
